TPU v7x, 32 devices: a whole 2x2x4 slice. The times are simulated.
32 devices in a mesh: group: 2 (over y), expert: 16 (over z, x, core).
Axes of the slice: x: 2, y: 2, z: 4, core: 2. Of those that a mesh axis runs over, the one named last changes fastest.
Arguments:
- tokens: bfloat16 [256, 7168], P(('group', 'expert')), parts along dimension 0, may hold values from -6 to 6
- expert_ids: int32 [256, 8], P(('group', 'expert')), parts along dimension 0, may hold values from 0 to 15, all different within a row; in each aligned block of 8 rows (0 to 7, 8 to 15, ...) at most 5 rows name the same one
- gate_probs: float32 [256, 8], P(('group', 'expert')), parts along dimension 0, may hold values from 0.05 to 0.6
- gate_proj: bfloat16 [7168, 32768], P(None, 'expert'), may hold values from -0.0625 to 0.0625
- up_proj: bfloat16 [7168, 32768], P(None, 'expert'), may hold values from -0.0625 to 0.0625
- down_proj: bfloat16 [32768, 7168], P('expert'), may hold values from -0.125 to 0.125
Outputs:
- mixed: bfloat16 [256, 7168], P(('group', 'expert')), parts along dimension 0
There are 2 independent parts, one for each index of `group`. A program takes and returns all parts, laid end to end along the dimension named above; an argument that names none is the same for every part. Nothing has to cross between parts.
Inputs may be any that keep to these rules, and one draw needn't show every extreme that they name: `expert_ids`: each row names 8 different experts. Among the 8 tokens of one device (aligned blocks of 8 rows) no expert is named by more than 5 tokens, a bound that some blocks reach.
All inputs are finite; a program needn't handle non-finite values.
Results may differ from a plain program's by a relative error of at most 0.0051.
Values may be sent and summed in bfloat16 or wider, within the bound.
No kernel may reach another device: no remote copies, remote signals or barrier semaphores. Data moves between devices by JAX's collectives and lax.ppermute only.
A program may use at most 192 MiB of HBM per device.

v0:
```python
import jax
import jax.numpy as jnp
from jax import lax
from jax.sharding import PartitionSpec as P

FF = 2048
EXPERTS = 16
CAP = 5


def shards(tokens, expert_ids, gate_probs, gate_proj, up_proj, down_proj):
    hid_count = gate_proj.shape[1]
    splits = FF // hid_count
    tok_count, model_width = tokens.shape
    devices = lax.axis_size("expert")
    picks = expert_ids[:, :, None] == jnp.arange(EXPERTS, dtype=jnp.int32)[None, None, :]
    chosen = jnp.sum(picks.astype(jnp.int32), axis=1)
    weight_te = jnp.sum(jnp.where(picks, gate_probs[:, :, None], 0.0), axis=1)
    slot_of = jnp.cumsum(chosen, axis=0) - 1
    placed = (chosen[:, :, None] == 1) & (
        slot_of[:, :, None] == jnp.arange(CAP, dtype=jnp.int32)[None, None, :]
    )
    picked = placed.astype(jnp.bfloat16)
    combine_w = jnp.where(placed, weight_te[:, :, None], 0.0)
    packed = jnp.einsum("tec,td->ecd", picked, tokens, preferred_element_type=jnp.float32).astype(
        jnp.bfloat16
    )
    outgoing = jnp.broadcast_to(packed[:, None], (EXPERTS, splits, CAP, model_width)).reshape(
        devices, CAP, model_width
    )
    blocks = lax.all_to_all(outgoing, "expert", split_axis=0, concat_axis=0, tiled=True)
    flat_rows = blocks.reshape(-1, model_width)
    gate_val = jnp.dot(flat_rows, gate_proj, preferred_element_type=jnp.float32)
    up_val = jnp.dot(flat_rows, up_proj, preferred_element_type=jnp.float32)
    hidden = (jax.nn.silu(gate_val) * up_val).astype(jnp.bfloat16)
    result = jnp.dot(hidden, down_proj, preferred_element_type=jnp.float32)
    partial_value = result.reshape(blocks.shape[0], blocks.shape[1], model_width)
    returned = lax.all_to_all(partial_value, "expert", split_axis=0, concat_axis=0, tiled=True)
    returned = returned.reshape(EXPERTS, splits, CAP, model_width)
    combined = jnp.einsum("tec,escd->td", combine_w, returned, precision=lax.Precision.HIGHEST)
    return combined.astype(jnp.bfloat16)


def solution(mesh):
    placed = (
        P(("group", "expert"), None),
        P(("group", "expert"), None),
        P(("group", "expert"), None),
        P(None, "expert"),
        P(None, "expert"),
        P("expert", None),
    )
    return jax.shard_map(
        shards, mesh=mesh, in_specs=placed, out_specs=P(("group", "expert"), None), check_vma=False
    )
```

profile of v0, /device:TPU:15, one launch (start us, length us, event | category | flops | bytes accessed | tf_op | source)
XLA Modules:
  0.0 180.2 jit_solution(9811228272586178524)
XLA Ops:
  0.0 0.0 copy-start
  0.0 0.8 convert_reduce_fusion
  0.8 0.0 copy-start.5
  0.9 0.0 copy-start.2
  0.9 0.6 copy-done.2
  1.5 0.0 copy-done
  1.5 0.5 convolution_convert_fusion
  2.0 0.7 copy.12
  2.6 0.0 copy-done.5
  2.6 48.0 %all_to_all.10 = bf16[16,5,7168]{2,1,0:T(8,128)(2,1)S(1)} all-to-all(bf16[16,5,7168]{2,1,0:T(8,128)(2,1)S(1)} %copy.12), channel_id=1, replica_groups=mesh['group'=2,'expert'=16] {'expert'}, dimensions={0} | all-to-all | bytes 2293760 | tf_op jit(solution)/shard_map/all_to_all | solution.py:31
  50.7 0.6 reshape.23
  51.2 12.9 %fusion.23 = f32[80,2048]{1,0:T(8,128)} fusion(bf16[80,7168]{1,0:T(8,128)(2,1)S(1)} %reshape.23, bf16[7168,2048]{1,0:T(8,128)(2,1)} %param.9), kind=kOutput, calls=%fused_computation.30 | convolution fusion | flops 2348810240 | bytes 31162368 | tf_op jit(solution)/shard_map/dot_general | solution.py:33
  64.1 21.0 %fusion.2 = f32[80,7168]{1,0:T(8,128)S(1)} fusion(bf16[2048,7168]{1,0:T(8,128)(2,1)} %param.11, bf16[80,7168]{1,0:T(8,128)(2,1)S(1)} %reshape.23, bf16[7168,2048]{1,0:T(8,128)(2,1)} %param.10, f32[80,2048]{1,0:T(8,128)} %fusion.23), kind=kOutput, calls=%fused_computation.5 | convolution fusion | flops 4698603520 | bytes 62816256 | tf_op jit(solution)/shard_map/dot_general | solution.py:36
  85.1 0.0 copy-start.1
  85.1 2.0 %reshape.24 = f32[16,5,7168]{2,1,0:T(8,128)} reshape(f32[80,7168]{1,0:T(8,128)S(1)} %fusion.2) | data formatting | bytes 4587520 | tf_op jit(solution)/shard_map/reshape | solution.py:37
  87.2 0.0 copy-start.4
  87.2 0.0 copy-start.7
  87.2 0.0 copy-start.3
  87.2 0.0 copy-start.6
  87.2 5.6 %all-to-all-start.1 = ((f32[16,5,7168]{2,1,0:T(8,128)}), f32[16,5,7168]{2,1,0:T(8,128)}, u32[]{:S(2)}, u32[]{:S(2)}) async-start(f32[16,5,7168]{2,1,0:T(8,128)} %reshape.24), calls=%async_computation.1 | async-start | bytes 7340032 | tf_op jit(solution)/shard_map/all_to_all | solution.py:38
  92.8 0.0 copy-done.4
  92.8 0.0 copy-done.7
  92.8 0.1 select_reduce_fusion
  92.9 81.1 %all-to-all-done.1 = f32[16,5,7168]{2,1,0:T(8,128)} async-done(((f32[16,5,7168]{2,1,0:T(8,128)}), f32[16,5,7168]{2,1,0:T(8,128)}, u32[]{:S(2)}, u32[]{:S(2)}) %all-to-all-start.1) | async-done | bytes 2293792 | tf_op jit(solution)/shard_map/all_to_all | solution.py:38
  174.0 0.0 copy-done.3
  174.0 0.0 copy-done.6
  174.0 6.2 %fusion = bf16[8,7168]{1,0:T(8,128)(2,1)} fusion(f32[16,5,7168]{2,1,0:T(8,128)} %all-to-all-done.1, f32[8,16]{1,0:T(8,128)S(1)} %select_reduce_fusion, s32[8,16]{1,0:T(8,128)S(1)} %copy-done.3, pred[8,16]{1,0:T(8,128)(4,1)S(1)} %copy-done.6), kind=kOutput, calls=%fused_computation.2 | convolution fusion | flops 55109504 | bytes 2409600 | tf_op jit(solution)/shard_map/tec,escd->td/dot_general | solution.py:40
  180.2 0.0 copy-done.1
  (3 shorter events, 0.0 us)
Async XLA Ops:
  0.0 1.5 copy-start
  0.8 1.8 copy-start.5
  0.9 0.6 copy-start.2
  85.1 95.1 %copy-start.1 = (bf16[8,7168]{1,0:T(8,128)(2,1)S(1)}, bf16[8,7168]{1,0:T(8,128)(2,1)}, u32[]{:S(2)}) copy-start(bf16[8,7168]{1,0:T(8,128)(2,1)} %param.6) | copy-start | bytes 344068
  87.2 5.6 %copy-start.4 = (s32[8,8]{1,0:T(8,128)S(1)}, s32[8,8]{1,0:T(8,128)}, u32[]{:S(2)}) copy-start(s32[8,8]{1,0:T(8,128)} %param.7) | copy-start | bytes 772
  87.2 5.6 %copy-start.7 = (f32[8,8]{1,0:T(8,128)S(1)}, f32[8,8]{1,0:T(8,128)}, u32[]{:S(2)}) copy-start(f32[8,8]{1,0:T(8,128)} %param.8) | copy-start | bytes 772
  87.2 86.8 %copy-start.3 = (s32[8,16]{1,0:T(8,128)S(1)}, s32[8,16]{1,0:T(8,128)}, u32[]{:S(2)}) copy-start(s32[8,16]{1,0:T(8,128)} %copy-done.2) | copy-start | bytes 1540
  87.2 86.8 %copy-start.6 = (pred[8,16]{1,0:T(8,128)(4,1)S(1)}, pred[8,16]{1,0:T(8,128)(4,1)}, u32[]{:S(2)}) copy-start(pred[8,16]{1,0:T(8,128)(4,1)} %copy-done.5) | copy-start | bytes 388
  87.2 86.8 %all-to-all-start.1 = ((f32[16,5,7168]{2,1,0:T(8,128)}), f32[16,5,7168]{2,1,0:T(8,128)}, u32[]{:S(2)}, u32[]{:S(2)}) async-start(f32[16,5,7168]{2,1,0:T(8,128)} %reshape.24), calls=%async_computation.1 | async-start | bytes 7340032 | tf_op jit(solution)/shard_map/all_to_all | solution.py:38
where the time goes:
time: 180 us
  waiting for transfers between devices  81.1 us (45%)
  blocking collectives  48 us (27%)
  matrix products  40.5 us (22%)
  starting transfers between devices  5.58 us (3%)
  local copies, waits for them, and re-layouts  3.86 us (2%)
    all_to_all x1, waiting for transfers between devices, shards(): lax.all_to_all(partial_value, 'expert', split_axis=0, concat_axis=0, tile...  81.1 us
    all_to_all x1, blocking collectives, shards(): lax.all_to_all(outgoing, 'expert', split_axis=0, concat_axis=0, tiled=True)  48 us
    dot_general x1, matrix products, shards(): result = jnp.dot(hidden, down_proj, preferred_element_type=jnp.float32)  21 us
    dot_general x1, matrix products, shards(): gate_val = jnp.dot(flat_rows, gate_proj, preferred_element_type=jnp.float32)  12.9 us
    dot_general x1, matrix products, shards(): jnp.einsum('tec,escd->td', combine_w, returned, precision=lax.Precision.H...  6.16 us
    all_to_all x1, starting transfers between devices, shards(): lax.all_to_all(partial_value, 'expert', split_axis=0, concat_axis=0, tile...  5.58 us
  transfers between devices with their start and end apart: 1, of which 1 were waited for; matrix products, arithmetic and copies ran while one was open for 0% of the time, Pallas kernels for 0%

commit v1 on v0

v1 whole, which is shorter than its diff:
```python
import jax
import jax.numpy as jnp
from jax import lax
from jax.sharding import PartitionSpec as P

FF = 2048
EXPERTS = 16
EXTRA = 128


def swap(value, bit, devices):
    return lax.ppermute(value, "expert", [(i, i ^ bit) for i in range(devices)])


def stages(devices):
    low = [1, 2]
    high = [b for b in range(4, devices, 4)]
    return low, high


def gather(block, devices):
    low, high = stages(devices)
    rows = [block] + [swap(block, b, devices) for b in high]
    rows = jnp.concatenate(rows, axis=0)
    for bit in reversed(low):
        rows = jnp.concatenate([rows, swap(rows, bit, devices)], axis=0)
    return rows


def order(devices):
    low, high = stages(devices)
    places = [0] + high
    for bit in reversed(low):
        places = places + [p ^ bit for p in places]
    return places


def scatter_sum(part, devices):
    low, high = stages(devices)
    for bit in low:
        half = part.shape[0] // 2
        got = swap(part[half:].astype(jnp.bfloat16), bit, devices)
        part = part[:half] + got.astype(jnp.float32)
    rows = part.shape[0] // (1 + len(high))
    total = part[:rows]
    sent = part[rows:].astype(jnp.bfloat16)
    for k, bit in enumerate(high):
        got = swap(sent[k * rows : (k + 1) * rows], bit, devices)
        total = total + got.astype(jnp.float32)
    return total


def shards(tokens, expert_ids, gate_probs, gate_proj, up_proj, down_proj):
    hid_count = gate_proj.shape[1]
    splits = FF // hid_count
    tok_count, model_width = tokens.shape
    devices = lax.axis_size("expert")
    own = lax.axis_index("expert") // splits
    picks = expert_ids[:, :, None] == jnp.arange(EXPERTS, dtype=jnp.int32)[None, None, :]
    weight_te = jnp.sum(jnp.where(picks, gate_probs[:, :, None], 0.0), axis=1)
    hi = lax.reduce_precision(weight_te, 8, 7)
    mid = lax.reduce_precision(weight_te - hi, 8, 7)
    lo = weight_te - hi - mid
    pad = jnp.zeros((tok_count, EXTRA - 3 * EXPERTS), jnp.float32)
    extra = jnp.concatenate([hi, mid, lo, pad], axis=1).astype(jnp.bfloat16)
    rows = gather(jnp.concatenate([tokens, extra], axis=1), devices)
    pieces = rows[:, model_width:].astype(jnp.float32)
    lane = jnp.arange(EXTRA, dtype=jnp.int32)[None, :]
    mine = (lane < 3 * EXPERTS) & (lane % EXPERTS == own)
    weight = jnp.sum(jnp.where(mine, pieces, 0.0), axis=1, keepdims=True)
    flat_rows = rows[:, :model_width]
    gate_val = jnp.dot(flat_rows, gate_proj, preferred_element_type=jnp.float32)
    up_val = jnp.dot(flat_rows, up_proj, preferred_element_type=jnp.float32)
    hidden = (jax.nn.silu(gate_val) * up_val).astype(jnp.bfloat16)
    outs = []
    chunks = 4
    width = model_width // chunks
    for k in range(chunks):
        part = jnp.dot(hidden, down_proj[:, k * width : (k + 1) * width], preferred_element_type=jnp.float32)
        outs.append(scatter_sum(part * weight, devices).astype(jnp.bfloat16))
    return jnp.concatenate(outs, axis=1)


def solution(mesh):
    placed = (
        P(("group", "expert"), None),
        P(("group", "expert"), None),
        P(("group", "expert"), None),
        P(None, "expert"),
        P(None, "expert"),
        P("expert", None),
    )
    return jax.shard_map(
        shards, mesh=mesh, in_specs=placed, out_specs=P(("group", "expert"), None), check_vma=False
    )
```

time: 180 us -> 107 us (0.59)
  the two profiles are of different devices: /device:TPU:15 before, /device:TPU:0 now
where the time goes in v1:
time: 107 us
  matrix products  42.1 us (39%)
  starting transfers between devices  33.1 us (31%)
  waiting for transfers between devices  24.3 us (23%)
  local copies, waits for them, and re-layouts  4.78 us (4%)
  other arithmetic  2.01 us (2%)
    ppermute x25, starting transfers between devices, swap(): return lax.ppermute(value, 'expert', [(i, i ^ bit) for i in range(devices)])  33.1 us
    ppermute x25, waiting for transfers between devices, swap(): return lax.ppermute(value, 'expert', [(i, i ^ bit) for i in range(devices)])  24.3 us
    dot_general x4, matrix products, shards(): jnp.dot(hidden, down_proj[:, k * width:(k + 1) * width], preferred_elemen...  16.9 us
    dot_general x1, matrix products, shards(): up_val = jnp.dot(flat_rows, up_proj, preferred_element_type=jnp.float32)  13.5 us
    dot_general x1, matrix products, shards(): gate_val = jnp.dot(flat_rows, gate_proj, preferred_element_type=jnp.float32)  11.6 us
    unnamed x4, local copies, waits for them, and re-layouts  2.64 us
  transfers between devices with their start and end apart: 25, of which 9 were waited for; matrix products, arithmetic and copies ran while one was open for 7% of the time, Pallas kernels for 0%

profile of v1, /device:TPU:0, one launch (start us, length us, event | category | flops | bytes accessed | tf_op | source)
XLA Modules:
  0.0 106.6 jit_solution(16521278400023781682)
XLA Ops:
  0.0 0.8 select_reduce_fusion.1
  0.8 1.0 concatenate.20
  1.8 3.0 %collective-permute-start = (bf16[8,7296]{1,0:T(8,128)(2,1)S(1)}, bf16[8,7296]{1,0:T(8,128)(2,1)S(1)}, u32[]{:S(2)}, u32[]{:S(2)}) collective-permute-start(bf16[8,7296]{1,0:T(8,128)(2,1)S(1)} %concatenate.20), channel_id=1, source_target_pairs={{0,4},{1,5},{2,6},{3,7},{4,0},{5,1},{6,2},{7,3},{8,12},{9,13},{10,... | collective-permute-start | bytes 350216 | tf_op jit(solution)/shard_map/ppermute | solution.py:12
  4.9 2.6 %collective-permute-start.1 = (bf16[8,7296]{1,0:T(8,128)(2,1)S(1)}, bf16[8,7296]{1,0:T(8,128)(2,1)S(1)}, u32[]{:S(2)}, u32[]{:S(2)}) collective-permute-start(bf16[8,7296]{1,0:T(8,128)(2,1)S(1)} %concatenate.20), channel_id=1, source_target_pairs={{0,8},{1,9},{2,10},{3,11},{4,12},{5,13},{6,14},{7,15},{8,0},{9,1},... | collective-permute-start | bytes 350216 | tf_op jit(solution)/shard_map/ppermute | solution.py:12
  7.4 0.7 constant_dynamic-update-slice_fusion.4
  8.1 1.2 %collective-permute-done = bf16[8,7296]{1,0:T(8,128)(2,1)S(1)} collective-permute-done((bf16[8,7296]{1,0:T(8,128)(2,1)S(1)}, bf16[8,7296]{1,0:T(8,128)(2,1)S(1)}, u32[]{:S(2)}, u32[]{:S(2)}) %collective-permute-start) | collective-permute-done | bytes 116768 | tf_op jit(solution)/shard_map/ppermute | solution.py:12
  9.3 7.4 %collective-permute-done.1 = bf16[8,7296]{1,0:T(8,128)(2,1)S(1)} collective-permute-done((bf16[8,7296]{1,0:T(8,128)(2,1)S(1)}, bf16[8,7296]{1,0:T(8,128)(2,1)S(1)}, u32[]{:S(2)}, u32[]{:S(2)}) %collective-permute-start.1) | collective-permute-done | bytes 116768 | tf_op jit(solution)/shard_map/ppermute | solution.py:12
  16.7 0.1 pad_maximum_fusion
  16.8 1.6 %collective-permute-start.3 = (bf16[32,7296]{1,0:T(8,128)(2,1)S(1)}, bf16[32,7296]{1,0:T(8,128)(2,1)S(1)}, u32[]{:S(2)}, u32[]{:S(2)}) collective-permute-start(bf16[32,7296]{1,0:T(8,128)(2,1)S(1)} %pad_maximum_fusion), channel_id=1, source_target_pairs={{0,2},{1,3},{2,0},{3,1},{4,6},{5,7},{6,4},{7,5},{8,10},{9,11},{10,... | collective-permute-start | bytes 1400840 | tf_op jit(solution)/shard_map/ppermute | solution.py:12
  18.3 0.6 constant_dynamic-update-slice_fusion.3
  19.0 0.7 constant_dynamic-update-slice_fusion.2
  19.6 0.7 constant_dynamic-update-slice_fusion.1
  20.3 6.7 %collective-permute-done.3 = bf16[32,7296]{1,0:T(8,128)(2,1)S(1)} collective-permute-done((bf16[32,7296]{1,0:T(8,128)(2,1)S(1)}, bf16[32,7296]{1,0:T(8,128)(2,1)S(1)}, u32[]{:S(2)}, u32[]{:S(2)}) %collective-permute-start.3) | collective-permute-done | bytes 466976 | tf_op jit(solution)/shard_map/ppermute | solution.py:12
  27.0 0.8 constant_dynamic-update-slice_fusion
  27.8 2.7 %collective-permute-done.4 = bf16[64,7296]{1,0:T(8,128)(2,1)S(1)} collective-permute-done((bf16[64,7296]{1,0:T(8,128)(2,1)}, bf16[64,7296]{1,0:T(8,128)(2,1)S(1)}, u32[]{:S(2)}, u32[]{:S(2)}) %collective-permute-start.4) | collective-permute-done | bytes 933920 | tf_op jit(solution)/shard_map/ppermute | solution.py:12
  30.5 0.1 constant_dynamic-update-slice_fusion.5
  30.6 11.6 %fusion.22 = f32[128,2048]{1,0:T(8,128)S(1)} fusion(bf16[7168,2048]{1,0:T(8,128)(2,1)} %param.9, bf16[128,7296]{1,0:T(8,128)(2,1)S(1)} %constant_dynamic-update-slice_fusion.5), kind=kOutput, calls=%fused_computation.14 | convolution fusion | flops 3758096384 | bytes 32243712 | tf_op jit(solution)/shard_map/dot_general | solution.py:72
  42.3 0.1 select_reduce_fusion
  42.4 13.5 %multiply_convert_fusion = bf16[128,2048]{1,0:T(8,128)(2,1)S(1)} fusion(f32[128,2048]{1,0:T(8,128)S(1)} %fusion.22, bf16[7168,2048]{1,0:T(8,128)(2,1)} %param.10, bf16[128,7296]{1,0:T(8,128)(2,1)S(1)} %constant_dynamic-update-slice_fusion.5), kind=kOutput, calls=%fused_computation.16 | convolution fusion | flops 3759669248 | bytes 32768000 | tf_op jit(solution)/shard_map/dot_general | solution.py:73
  55.9 4.2 %fusion.8 = f32[128,1792]{1,0:T(8,128)S(1)} fusion(bf16[128,2048]{1,0:T(8,128)(2,1)S(1)} %multiply_convert_fusion, bf16[2048,7168]{1,0:T(8,128)(2,1)} %param.11, f32[128]{0:T(128)S(1)} %select_reduce_fusion), kind=kOutput, calls=%fused_computation.8 | convolution fusion | flops 939753472 | bytes 8782336 | tf_op jit(solution)/shard_map/dot_general | solution.py:79
  60.1 4.2 %fusion.11 = f32[128,1792]{1,0:T(8,128)S(1)} fusion(bf16[128,2048]{1,0:T(8,128)(2,1)S(1)} %multiply_convert_fusion, bf16[2048,7168]{1,0:T(8,128)(2,1)} %param.11, f32[128]{0:T(128)S(1)} %select_reduce_fusion), kind=kOutput, calls=%fused_computation.9 | convolution fusion | flops 939753472 | bytes 8782336 | tf_op jit(solution)/shard_map/dot_general | solution.py:79
  64.4 4.2 %fusion.14 = f32[128,1792]{1,0:T(8,128)S(1)} fusion(bf16[128,2048]{1,0:T(8,128)(2,1)S(1)} %multiply_convert_fusion, bf16[2048,7168]{1,0:T(8,128)(2,1)} %param.11, f32[128]{0:T(128)S(1)} %select_reduce_fusion), kind=kOutput, calls=%fused_computation.10 | convolution fusion | flops 939753472 | bytes 8782336 | tf_op jit(solution)/shard_map/dot_general | solution.py:79
  68.6 0.2 collective-permute-start.5
  68.8 4.2 %fusion.17 = f32[128,1792]{1,0:T(8,128)S(1)} fusion(bf16[128,2048]{1,0:T(8,128)(2,1)S(1)} %multiply_convert_fusion, bf16[2048,7168]{1,0:T(8,128)(2,1)} %param.11, f32[128]{0:T(128)S(1)} %select_reduce_fusion), kind=kOutput, calls=%fused_computation.11 | convolution fusion | flops 939753472 | bytes 8782336 | tf_op jit(solution)/shard_map/dot_general | solution.py:79
  73.1 0.4 collective-permute-start.10
  73.6 0.2 collective-permute-start.15
  73.8 0.4 collective-permute-start.20
  74.3 1.6 %collective-permute-start.6 = (bf16[32,1792]{1,0:T(8,128)(2,1)S(1)}, bf16[32,1792]{1,0:T(8,128)(2,1)S(1)}, u32[]{:S(2)}, u32[]{:S(2)}) collective-permute-start(bf16[32,1792]{1,0:T(8,128)(2,1)S(1)} %slice.286), channel_id=1, source_target_pairs={{0,2},{1,3},{2,0},{3,1},{4,6},{5,7},{6,4},{7,5},{8,10},{9,11},{10,... | collective-permute-start | bytes 344072 | tf_op jit(solution)/shard_map/ppermute | solution.py:12
  75.9 0.1 slice_add_fusion.2
  76.0 0.6 collective-permute-start.11
  76.6 1.6 %collective-permute-start.16 = (bf16[32,1792]{1,0:T(8,128)(2,1)S(1)}, bf16[32,1792]{1,0:T(8,128)(2,1)S(1)}, u32[]{:S(2)}, u32[]{:S(2)}) collective-permute-start(bf16[32,1792]{1,0:T(8,128)(2,1)S(1)} %slice.284), channel_id=1, source_target_pairs={{0,2},{1,3},{2,0},{3,1},{4,6},{5,7},{6,4},{7,5},{8,10},{9,11},{10,... | collective-permute-start | bytes 344072 | tf_op jit(solution)/shard_map/ppermute | solution.py:12
  78.3 0.6 collective-permute-start.21
  78.9 1.5 %collective-permute-done.6 = bf16[32,1792]{1,0:T(8,128)(2,1)S(1)} collective-permute-done((bf16[32,1792]{1,0:T(8,128)(2,1)S(1)}, bf16[32,1792]{1,0:T(8,128)(2,1)S(1)}, u32[]{:S(2)}, u32[]{:S(2)}) %collective-permute-start.6) | collective-permute-done | bytes 114720 | tf_op jit(solution)/shard_map/ppermute | solution.py:12
  80.4 2.8 %collective-permute-start.7 = (bf16[8,1792]{1,0:T(8,128)(2,1)S(1)}, bf16[8,1792]{1,0:T(8,128)(2,1)S(1)}, u32[]{:S(2)}, u32[]{:S(2)}) collective-permute-start(bf16[8,1792]{1,0:T(8,128)(2,1)S(1)} %get-tuple-element.23), channel_id=1, source_target_pairs={{0,4},{1,5},{2,6},{3,7},{4,0},{5,1},{6,2},{7,3},{8,12},{9,13},{10,... | collective-permute-start | bytes 86024 | tf_op jit(solution)/shard_map/ppermute | solution.py:12
  83.3 1.4 %collective-permute-start.8 = (bf16[8,1792]{1,0:T(8,128)(2,1)S(1)}, bf16[8,1792]{1,0:T(8,128)(2,1)S(1)}, u32[]{:S(2)}, u32[]{:S(2)}) collective-permute-start(bf16[8,1792]{1,0:T(8,128)(2,1)S(1)} %get-tuple-element.25), channel_id=1, source_target_pairs={{0,8},{1,9},{2,10},{3,11},{4,12},{5,13},{6,14},{7,15},{8,0},{9,1},... | collective-permute-start | bytes 86024 | tf_op jit(solution)/shard_map/ppermute | solution.py:12
  84.7 1.4 %collective-permute-start.9 = (bf16[8,1792]{1,0:T(8,128)(2,1)S(1)}, bf16[8,1792]{1,0:T(8,128)(2,1)S(1)}, u32[]{:S(2)}, u32[]{:S(2)}) collective-permute-start(bf16[8,1792]{1,0:T(8,128)(2,1)S(1)} %get-tuple-element.24), channel_id=1, source_target_pairs={{0,12},{1,13},{2,14},{3,15},{4,8},{5,9},{6,10},{7,11},{8,4},{9,5},... | collective-permute-start | bytes 86024 | tf_op jit(solution)/shard_map/ppermute | solution.py:12
  86.2 1.9 %collective-permute-start.12 = (bf16[8,1792]{1,0:T(8,128)(2,1)S(1)}, bf16[8,1792]{1,0:T(8,128)(2,1)S(1)}, u32[]{:S(2)}, u32[]{:S(2)}) collective-permute-start(bf16[8,1792]{1,0:T(8,128)(2,1)S(1)} %get-tuple-element.26), channel_id=1, source_target_pairs={{0,4},{1,5},{2,6},{3,7},{4,0},{5,1},{6,2},{7,3},{8,12},{9,13},{10,... | collective-permute-start | bytes 86024 | tf_op jit(solution)/shard_map/ppermute | solution.py:12
  88.1 3.0 %collective-permute-start.13 = (bf16[8,1792]{1,0:T(8,128)(2,1)S(1)}, bf16[8,1792]{1,0:T(8,128)(2,1)S(1)}, u32[]{:S(2)}, u32[]{:S(2)}) collective-permute-start(bf16[8,1792]{1,0:T(8,128)(2,1)S(1)} %get-tuple-element.28), channel_id=1, source_target_pairs={{0,8},{1,9},{2,10},{3,11},{4,12},{5,13},{6,14},{7,15},{8,0},{9,1},... | collective-permute-start | bytes 86024 | tf_op jit(solution)/shard_map/ppermute | solution.py:12
  91.2 1.1 collective-permute-start.14
  92.2 3.4 %collective-permute-start.18 = (bf16[8,1792]{1,0:T(8,128)(2,1)S(1)}, bf16[8,1792]{1,0:T(8,128)(2,1)S(1)}, u32[]{:S(2)}, u32[]{:S(2)}) collective-permute-start(bf16[8,1792]{1,0:T(8,128)(2,1)S(1)} %get-tuple-element.31), channel_id=1, source_target_pairs={{0,8},{1,9},{2,10},{3,11},{4,12},{5,13},{6,14},{7,15},{8,0},{9,1},... | collective-permute-start | bytes 86024 | tf_op jit(solution)/shard_map/ppermute | solution.py:12
  95.7 1.1 collective-permute-start.19
  96.7 0.2 collective-permute-done.14
  96.9 3.2 %collective-permute-start.23 = (bf16[8,1792]{1,0:T(8,128)(2,1)S(1)}, bf16[8,1792]{1,0:T(8,128)(2,1)S(1)}, u32[]{:S(2)}, u32[]{:S(2)}) collective-permute-start(bf16[8,1792]{1,0:T(8,128)(2,1)S(1)} %get-tuple-element.34), channel_id=1, source_target_pairs={{0,8},{1,9},{2,10},{3,11},{4,12},{5,13},{6,14},{7,15},{8,0},{9,1},... | collective-permute-start | bytes 86024 | tf_op jit(solution)/shard_map/ppermute | solution.py:12
  100.2 1.0 collective-permute-start.24
  101.2 0.2 collective-permute-done.19
  101.4 0.5 collective-permute-done.23
  102.0 3.9 %collective-permute-done.24 = bf16[8,1792]{1,0:T(8,128)(2,1)S(1)} collective-permute-done((bf16[8,1792]{1,0:T(8,128)(2,1)S(1)}, bf16[8,1792]{1,0:T(8,128)(2,1)S(1)}, u32[]{:S(2)}, u32[]{:S(2)}) %collective-permute-start.24) | collective-permute-done | bytes 28704 | tf_op jit(solution)/shard_map/ppermute | solution.py:12
  105.9 0.7 pad_maximum_fusion.1
  (46 shorter events, 0.6 us)
Async XLA Ops:
  1.8 7.4 %collective-permute-start = (bf16[8,7296]{1,0:T(8,128)(2,1)S(1)}, bf16[8,7296]{1,0:T(8,128)(2,1)S(1)}, u32[]{:S(2)}, u32[]{:S(2)}) collective-permute-start(bf16[8,7296]{1,0:T(8,128)(2,1)S(1)} %concatenate.20), channel_id=1, source_target_pairs={{0,4},{1,5},{2,6},{3,7},{4,0},{5,1},{6,2},{7,3},{8,12},{9,13},{10,... | collective-permute-start | bytes 350216 | tf_op jit(solution)/shard_map/ppermute | solution.py:12
  4.9 11.8 %collective-permute-start.1 = (bf16[8,7296]{1,0:T(8,128)(2,1)S(1)}, bf16[8,7296]{1,0:T(8,128)(2,1)S(1)}, u32[]{:S(2)}, u32[]{:S(2)}) collective-permute-start(bf16[8,7296]{1,0:T(8,128)(2,1)S(1)} %concatenate.20), channel_id=1, source_target_pairs={{0,8},{1,9},{2,10},{3,11},{4,12},{5,13},{6,14},{7,15},{8,0},{9,1},... | collective-permute-start | bytes 350216 | tf_op jit(solution)/shard_map/ppermute | solution.py:12
  7.4 9.3 %collective-permute-start.2 = (bf16[8,7296]{1,0:T(8,128)(2,1)S(1)}, bf16[8,7296]{1,0:T(8,128)(2,1)S(1)}, u32[]{:S(2)}, u32[]{:S(2)}) collective-permute-start(bf16[8,7296]{1,0:T(8,128)(2,1)S(1)} %concatenate.20), channel_id=1, source_target_pairs={{0,12},{1,13},{2,14},{3,15},{4,8},{5,9},{6,10},{7,11},{8,4},{9,5},... | collective-permute-start | bytes 350216 | tf_op jit(solution)/shard_map/ppermute | solution.py:12
  16.8 10.2 %collective-permute-start.3 = (bf16[32,7296]{1,0:T(8,128)(2,1)S(1)}, bf16[32,7296]{1,0:T(8,128)(2,1)S(1)}, u32[]{:S(2)}, u32[]{:S(2)}) collective-permute-start(bf16[32,7296]{1,0:T(8,128)(2,1)S(1)} %pad_maximum_fusion), channel_id=1, source_target_pairs={{0,2},{1,3},{2,0},{3,1},{4,6},{5,7},{6,4},{7,5},{8,10},{9,11},{10,... | collective-permute-start | bytes 1400840 | tf_op jit(solution)/shard_map/ppermute | solution.py:12
  27.8 2.7 %collective-permute-start.4 = (bf16[64,7296]{1,0:T(8,128)(2,1)}, bf16[64,7296]{1,0:T(8,128)(2,1)S(1)}, u32[]{:S(2)}, u32[]{:S(2)}) collective-permute-start(bf16[64,7296]{1,0:T(8,128)(2,1)} %get-tuple-element.13), channel_id=1, source_target_pairs={{0,1},{1,0},{2,3},{3,2},{4,5},{5,4},{6,7},{7,6},{8,9},{9,8},{10,11... | collective-permute-start | bytes 2801672 | tf_op jit(solution)/shard_map/ppermute | solution.py:12
  68.6 5.6 %collective-permute-start.5 = (bf16[64,1792]{1,0:T(8,128)(2,1)S(1)}, bf16[64,1792]{1,0:T(8,128)(2,1)S(1)}, u32[]{:S(2)}, u32[]{:S(2)}) collective-permute-start(bf16[64,1792]{1,0:T(8,128)(2,1)S(1)} %slice.282), channel_id=1, source_target_pairs={{0,1},{1,0},{2,3},{3,2},{4,5},{5,4},{6,7},{7,6},{8,9},{9,8},{10,11... | collective-permute-start | bytes 688136 | tf_op jit(solution)/shard_map/ppermute | solution.py:12
  73.1 2.8 %collective-permute-start.10 = (bf16[64,1792]{1,0:T(8,128)(2,1)S(1)}, bf16[64,1792]{1,0:T(8,128)(2,1)S(1)}, u32[]{:S(2)}, u32[]{:S(2)}) collective-permute-start(bf16[64,1792]{1,0:T(8,128)(2,1)S(1)} %slice.281), channel_id=1, source_target_pairs={{0,1},{1,0},{2,3},{3,2},{4,5},{5,4},{6,7},{7,6},{8,9},{9,8},{10,11... | collective-permute-start | bytes 688136 | tf_op jit(solution)/shard_map/ppermute | solution.py:12
  73.6 3.0 %collective-permute-start.15 = (bf16[64,1792]{1,0:T(8,128)(2,1)S(1)}, bf16[64,1792]{1,0:T(8,128)(2,1)S(1)}, u32[]{:S(2)}, u32[]{:S(2)}) collective-permute-start(bf16[64,1792]{1,0:T(8,128)(2,1)S(1)} %slice.280), channel_id=1, source_target_pairs={{0,1},{1,0},{2,3},{3,2},{4,5},{5,4},{6,7},{7,6},{8,9},{9,8},{10,11... | collective-permute-start | bytes 688136 | tf_op jit(solution)/shard_map/ppermute | solution.py:12
  73.8 4.4 %collective-permute-start.20 = (bf16[64,1792]{1,0:T(8,128)(2,1)S(1)}, bf16[64,1792]{1,0:T(8,128)(2,1)S(1)}, u32[]{:S(2)}, u32[]{:S(2)}) collective-permute-start(bf16[64,1792]{1,0:T(8,128)(2,1)S(1)} %slice.279), channel_id=1, source_target_pairs={{0,1},{1,0},{2,3},{3,2},{4,5},{5,4},{6,7},{7,6},{8,9},{9,8},{10,11... | collective-permute-start | bytes 688136 | tf_op jit(solution)/shard_map/ppermute | solution.py:12
  74.3 6.1 %collective-permute-start.6 = (bf16[32,1792]{1,0:T(8,128)(2,1)S(1)}, bf16[32,1792]{1,0:T(8,128)(2,1)S(1)}, u32[]{:S(2)}, u32[]{:S(2)}) collective-permute-start(bf16[32,1792]{1,0:T(8,128)(2,1)S(1)} %slice.286), channel_id=1, source_target_pairs={{0,2},{1,3},{2,0},{3,1},{4,6},{5,7},{6,4},{7,5},{8,10},{9,11},{10,... | collective-permute-start | bytes 344072 | tf_op jit(solution)/shard_map/ppermute | solution.py:12
  76.0 8.8 %collective-permute-start.11 = (bf16[32,1792]{1,0:T(8,128)(2,1)S(1)}, bf16[32,1792]{1,0:T(8,128)(2,1)S(1)}, u32[]{:S(2)}, u32[]{:S(2)}) collective-permute-start(bf16[32,1792]{1,0:T(8,128)(2,1)S(1)} %slice.285), channel_id=1, source_target_pairs={{0,2},{1,3},{2,0},{3,1},{4,6},{5,7},{6,4},{7,5},{8,10},{9,11},{10,... | collective-permute-start | bytes 344072 | tf_op jit(solution)/shard_map/ppermute | solution.py:12
  76.6 9.5 %collective-permute-start.16 = (bf16[32,1792]{1,0:T(8,128)(2,1)S(1)}, bf16[32,1792]{1,0:T(8,128)(2,1)S(1)}, u32[]{:S(2)}, u32[]{:S(2)}) collective-permute-start(bf16[32,1792]{1,0:T(8,128)(2,1)S(1)} %slice.284), channel_id=1, source_target_pairs={{0,2},{1,3},{2,0},{3,1},{4,6},{5,7},{6,4},{7,5},{8,10},{9,11},{10,... | collective-permute-start | bytes 344072 | tf_op jit(solution)/shard_map/ppermute | solution.py:12
  78.3 9.8 %collective-permute-start.21 = (bf16[32,1792]{1,0:T(8,128)(2,1)S(1)}, bf16[32,1792]{1,0:T(8,128)(2,1)S(1)}, u32[]{:S(2)}, u32[]{:S(2)}) collective-permute-start(bf16[32,1792]{1,0:T(8,128)(2,1)S(1)} %slice.283), channel_id=1, source_target_pairs={{0,2},{1,3},{2,0},{3,1},{4,6},{5,7},{6,4},{7,5},{8,10},{9,11},{10,... | collective-permute-start | bytes 344072 | tf_op jit(solution)/shard_map/ppermute | solution.py:12
  80.4 10.7 %collective-permute-start.7 = (bf16[8,1792]{1,0:T(8,128)(2,1)S(1)}, bf16[8,1792]{1,0:T(8,128)(2,1)S(1)}, u32[]{:S(2)}, u32[]{:S(2)}) collective-permute-start(bf16[8,1792]{1,0:T(8,128)(2,1)S(1)} %get-tuple-element.23), channel_id=1, source_target_pairs={{0,4},{1,5},{2,6},{3,7},{4,0},{5,1},{6,2},{7,3},{8,12},{9,13},{10,... | collective-permute-start | bytes 86024 | tf_op jit(solution)/shard_map/ppermute | solution.py:12
  83.3 8.9 %collective-permute-start.8 = (bf16[8,1792]{1,0:T(8,128)(2,1)S(1)}, bf16[8,1792]{1,0:T(8,128)(2,1)S(1)}, u32[]{:S(2)}, u32[]{:S(2)}) collective-permute-start(bf16[8,1792]{1,0:T(8,128)(2,1)S(1)} %get-tuple-element.25), channel_id=1, source_target_pairs={{0,8},{1,9},{2,10},{3,11},{4,12},{5,13},{6,14},{7,15},{8,0},{9,1},... | collective-permute-start | bytes 86024 | tf_op jit(solution)/shard_map/ppermute | solution.py:12
  84.7 7.5 %collective-permute-start.9 = (bf16[8,1792]{1,0:T(8,128)(2,1)S(1)}, bf16[8,1792]{1,0:T(8,128)(2,1)S(1)}, u32[]{:S(2)}, u32[]{:S(2)}) collective-permute-start(bf16[8,1792]{1,0:T(8,128)(2,1)S(1)} %get-tuple-element.24), channel_id=1, source_target_pairs={{0,12},{1,13},{2,14},{3,15},{4,8},{5,9},{6,10},{7,11},{8,4},{9,5},... | collective-permute-start | bytes 86024 | tf_op jit(solution)/shard_map/ppermute | solution.py:12
  86.2 9.5 %collective-permute-start.12 = (bf16[8,1792]{1,0:T(8,128)(2,1)S(1)}, bf16[8,1792]{1,0:T(8,128)(2,1)S(1)}, u32[]{:S(2)}, u32[]{:S(2)}) collective-permute-start(bf16[8,1792]{1,0:T(8,128)(2,1)S(1)} %get-tuple-element.26), channel_id=1, source_target_pairs={{0,4},{1,5},{2,6},{3,7},{4,0},{5,1},{6,2},{7,3},{8,12},{9,13},{10,... | collective-permute-start | bytes 86024 | tf_op jit(solution)/shard_map/ppermute | solution.py:12
  88.1 8.6 %collective-permute-start.13 = (bf16[8,1792]{1,0:T(8,128)(2,1)S(1)}, bf16[8,1792]{1,0:T(8,128)(2,1)S(1)}, u32[]{:S(2)}, u32[]{:S(2)}) collective-permute-start(bf16[8,1792]{1,0:T(8,128)(2,1)S(1)} %get-tuple-element.28), channel_id=1, source_target_pairs={{0,8},{1,9},{2,10},{3,11},{4,12},{5,13},{6,14},{7,15},{8,0},{9,1},... | collective-permute-start | bytes 86024 | tf_op jit(solution)/shard_map/ppermute | solution.py:12
  91.2 5.7 %collective-permute-start.14 = (bf16[8,1792]{1,0:T(8,128)(2,1)S(1)}, bf16[8,1792]{1,0:T(8,128)(2,1)S(1)}, u32[]{:S(2)}, u32[]{:S(2)}) collective-permute-start(bf16[8,1792]{1,0:T(8,128)(2,1)S(1)} %get-tuple-element.27), channel_id=1, source_target_pairs={{0,12},{1,13},{2,14},{3,15},{4,8},{5,9},{6,10},{7,11},{8,4},{9,5},... | collective-permute-start | bytes 86024 | tf_op jit(solution)/shard_map/ppermute | solution.py:12
  92.2 7.9 %collective-permute-start.17 = (bf16[8,1792]{1,0:T(8,128)(2,1)S(1)}, bf16[8,1792]{1,0:T(8,128)(2,1)S(1)}, u32[]{:S(2)}, u32[]{:S(2)}) collective-permute-start(bf16[8,1792]{1,0:T(8,128)(2,1)S(1)} %get-tuple-element.29), channel_id=1, source_target_pairs={{0,4},{1,5},{2,6},{3,7},{4,0},{5,1},{6,2},{7,3},{8,12},{9,13},{10,... | collective-permute-start | bytes 86024 | tf_op jit(solution)/shard_map/ppermute | solution.py:12
  92.2 9.0 %collective-permute-start.18 = (bf16[8,1792]{1,0:T(8,128)(2,1)S(1)}, bf16[8,1792]{1,0:T(8,128)(2,1)S(1)}, u32[]{:S(2)}, u32[]{:S(2)}) collective-permute-start(bf16[8,1792]{1,0:T(8,128)(2,1)S(1)} %get-tuple-element.31), channel_id=1, source_target_pairs={{0,8},{1,9},{2,10},{3,11},{4,12},{5,13},{6,14},{7,15},{8,0},{9,1},... | collective-permute-start | bytes 86024 | tf_op jit(solution)/shard_map/ppermute | solution.py:12
  95.7 5.7 %collective-permute-start.19 = (bf16[8,1792]{1,0:T(8,128)(2,1)S(1)}, bf16[8,1792]{1,0:T(8,128)(2,1)S(1)}, u32[]{:S(2)}, u32[]{:S(2)}) collective-permute-start(bf16[8,1792]{1,0:T(8,128)(2,1)S(1)} %get-tuple-element.30), channel_id=1, source_target_pairs={{0,12},{1,13},{2,14},{3,15},{4,8},{5,9},{6,10},{7,11},{8,4},{9,5},... | collective-permute-start | bytes 86024 | tf_op jit(solution)/shard_map/ppermute | solution.py:12
  96.7 4.7 %collective-permute-start.22 = (bf16[8,1792]{1,0:T(8,128)(2,1)S(1)}, bf16[8,1792]{1,0:T(8,128)(2,1)S(1)}, u32[]{:S(2)}, u32[]{:S(2)}) collective-permute-start(bf16[8,1792]{1,0:T(8,128)(2,1)S(1)} %get-tuple-element.32), channel_id=1, source_target_pairs={{0,4},{1,5},{2,6},{3,7},{4,0},{5,1},{6,2},{7,3},{8,12},{9,13},{10,... | collective-permute-start | bytes 86024 | tf_op jit(solution)/shard_map/ppermute | solution.py:12
  96.9 5.1 %collective-permute-start.23 = (bf16[8,1792]{1,0:T(8,128)(2,1)S(1)}, bf16[8,1792]{1,0:T(8,128)(2,1)S(1)}, u32[]{:S(2)}, u32[]{:S(2)}) collective-permute-start(bf16[8,1792]{1,0:T(8,128)(2,1)S(1)} %get-tuple-element.34), channel_id=1, source_target_pairs={{0,8},{1,9},{2,10},{3,11},{4,12},{5,13},{6,14},{7,15},{8,0},{9,1},... | collective-permute-start | bytes 86024 | tf_op jit(solution)/shard_map/ppermute | solution.py:12
  100.2 5.7 %collective-permute-start.24 = (bf16[8,1792]{1,0:T(8,128)(2,1)S(1)}, bf16[8,1792]{1,0:T(8,128)(2,1)S(1)}, u32[]{:S(2)}, u32[]{:S(2)}) collective-permute-start(bf16[8,1792]{1,0:T(8,128)(2,1)S(1)} %get-tuple-element.33), channel_id=1, source_target_pairs={{0,12},{1,13},{2,14},{3,15},{4,8},{5,9},{6,10},{7,11},{8,4},{9,5},... | collective-permute-start | bytes 86024 | tf_op jit(solution)/shard_map/ppermute | solution.py:12

commit v2 on v0

v2 whole, which is shorter than its diff:
```python
import functools

import jax
import jax.numpy as jnp
from jax import lax
from jax.experimental import pallas as pl
from jax.experimental.pallas import tpu as pltpu
from jax.sharding import PartitionSpec as P

FF = 2048
EXPERTS = 16
EXTRA = 128
F32 = jnp.float32
BF16 = jnp.bfloat16


def swap(value, bit, devices):
    return lax.ppermute(value, "expert", [(i, i ^ bit) for i in range(devices)])


def bit_order(devices):
    return [1 << k for k in reversed(range(devices.bit_length() - 1))]


def places_of(bits):
    places = [0]
    for bit in bits:
        places = places + [p ^ bit for p in places]
    return places


def reorder(rows, have, want, height):
    if have == want:
        return rows
    runs, start = [], 0
    spots = [have.index(p) for p in want]
    for k in range(1, len(spots) + 1):
        if k == len(spots) or spots[k] != spots[k - 1] + 1:
            runs.append((spots[start], spots[k - 1] + 1))
            start = k
    return jnp.concatenate([rows[a * height : b * height] for a, b in runs], axis=0)


def hid_kernel(rows, slots, own_ref, a0_ref, a1_ref, b0_ref, b1_ref, g_hbm, u_hbm, o_ref, w_ref, gbuf, ubuf, gacc, uacc, sems):
    kc = gbuf.shape[1]
    steps = g_hbm.shape[0] // kc
    first = a0_ref.shape[1] // kc
    half = rows // 2

    def copies(s):
        slot = s % slots
        src = pl.ds(s * kc, kc)
        return (
            pltpu.make_async_copy(g_hbm.at[src, :], gbuf.at[slot], sems.at[0, slot]),
            pltpu.make_async_copy(u_hbm.at[src, :], ubuf.at[slot], sems.at[1, slot]),
        )

    for s in range(min(slots, steps)):
        for copy in copies(s):
            copy.start()
    width = b0_ref.shape[1] - EXTRA
    lane = lax.broadcasted_iota(jnp.int32, (half, EXTRA), 1)
    mine = (lane < 3 * EXPERTS) & (lane % EXPERTS == own_ref[0])
    for k, ref in enumerate((b0_ref, b1_ref)):
        pieces = jnp.where(mine, ref[:, width:].astype(F32), 0.0)
        total = jnp.sum(pieces, axis=1, keepdims=True)
        w_ref[k * half : (k + 1) * half, :] = jnp.broadcast_to(total, (half, EXTRA))
    for s in range(steps):
        slot = s % slots
        top, low = (a0_ref, a1_ref) if s < first else (b0_ref, b1_ref)
        cols = slice((s % first) * kc, (s % first + 1) * kc)
        x = jnp.concatenate([top[:, cols], low[:, cols]], axis=0)
        for copy, buf, acc in zip(copies(s), (gbuf, ubuf), (gacc, uacc)):
            copy.wait()
            part = jnp.dot(x, buf[slot], preferred_element_type=F32)
            if s == 0:
                acc[...] = part
            else:
                acc[...] += part
        if s + slots < steps:
            for copy in copies(s + slots):
                copy.start()
    gate = gacc[...]
    o_ref[...] = (gate / (1.0 + jnp.exp(-gate)) * uacc[...]).astype(BF16)


def hidden_call(own, tops, lows, gate_proj, up_proj):
    model_width, hid = gate_proj.shape
    rows = 2 * tops[0].shape[0]
    kc, slots = 896, 3
    vmem = pl.BlockSpec(memory_space=pltpu.VMEM)
    anys = pl.BlockSpec(memory_space=pl.ANY)
    return pl.pallas_call(
        functools.partial(hid_kernel, rows, slots),
        name="gate_up",
        out_shape=(jax.ShapeDtypeStruct((rows, hid), BF16), jax.ShapeDtypeStruct((rows, EXTRA), F32)),
        in_specs=[pl.BlockSpec(memory_space=pltpu.SMEM)] + [vmem] * 4 + [anys] * 2,
        out_specs=(vmem, vmem),
        scratch_shapes=[
            pltpu.VMEM((slots, kc, hid), BF16),
            pltpu.VMEM((slots, kc, hid), BF16),
            pltpu.VMEM((rows, hid), F32),
            pltpu.VMEM((rows, hid), F32),
            pltpu.SemaphoreType.DMA((2, slots)),
        ],
        compiler_params=pltpu.CompilerParams(vmem_limit_bytes=50 << 20),
        cost_estimate=pl.CostEstimate(
            flops=4 * rows * model_width * hid, transcendentals=rows * hid, bytes_accessed=4 * model_width * hid
        ),
    )(own, tops[0], lows[0], tops[1], lows[1], gate_proj, up_proj)


def down_kernel(offset, slots, h_ref, w_ref, d_hbm, keep_ref, send_ref, buf, sems):
    nc = buf.shape[2]
    steps = keep_ref.shape[1] // nc
    half = keep_ref.shape[0]

    def copy(s):
        slot = s % slots
        return pltpu.make_async_copy(d_hbm.at[:, pl.ds(offset + s * nc, nc)], buf.at[slot], sems.at[slot])

    for s in range(min(slots, steps)):
        copy(s).start()
    weight = w_ref[:, 0:1]
    for s in range(steps):
        copy(s).wait()
        part = jnp.dot(h_ref[...], buf[s % slots], preferred_element_type=F32) * weight
        if s + slots < steps:
            copy(s + slots).start()
        keep_ref[:, s * nc : (s + 1) * nc] = part[:half]
        send_ref[:, s * nc : (s + 1) * nc] = part[half:].astype(BF16)


def down_call(hidden, weight, down_proj, offset, width):
    rows, hid = hidden.shape
    half = rows // 2
    nc, slots = 512, 5
    vmem = pl.BlockSpec(memory_space=pltpu.VMEM)
    return pl.pallas_call(
        functools.partial(down_kernel, offset, slots),
        name="down_" + str(offset),
        out_shape=(jax.ShapeDtypeStruct((half, width), F32), jax.ShapeDtypeStruct((half, width), BF16)),
        in_specs=[vmem, vmem, pl.BlockSpec(memory_space=pl.ANY)],
        out_specs=(vmem, vmem),
        scratch_shapes=[pltpu.VMEM((slots, hid, nc), BF16), pltpu.SemaphoreType.DMA((slots,))],
        compiler_params=pltpu.CompilerParams(vmem_limit_bytes=50 << 20),
        cost_estimate=pl.CostEstimate(
            flops=2 * rows * hid * width, transcendentals=0, bytes_accessed=2 * hid * width
        ),
    )(hidden, weight, down_proj)


def shards(tokens, expert_ids, gate_probs, gate_proj, up_proj, down_proj):
    splits = FF // gate_proj.shape[1]
    height, model_width = tokens.shape
    devices = lax.axis_size("expert")
    own = (lax.axis_index("expert") // splits).astype(jnp.int32).reshape(1)
    picks = expert_ids[:, :, None] == jnp.arange(EXPERTS, dtype=jnp.int32)[None, None, :]
    weight_te = jnp.sum(jnp.where(picks, gate_probs[:, :, None], 0.0), axis=1)
    hi = lax.reduce_precision(weight_te, 8, 7)
    mid = lax.reduce_precision(weight_te - hi, 8, 7)
    lo = weight_te - hi - mid
    pad = jnp.zeros((height, EXTRA - 3 * EXPERTS), F32)
    extra = jnp.concatenate([hi, mid, lo, pad], axis=1).astype(BF16)
    block = jnp.concatenate([tokens, extra], axis=1)

    bits = bit_order(devices)
    order_a = bits[:-1]
    order_b = bits[:-3] + [bits[-2], bits[-3]]
    rows = block
    for bit in order_a[:-2]:
        rows = jnp.concatenate([rows, swap(rows, bit, devices)], axis=0)
    width = model_width // 2
    part_a, part_b = rows[:, :width], rows[:, width:]
    for bit_a, bit_b in zip(order_a[-2:], order_b[-2:]):
        got_a, got_b = swap(part_a, bit_a, devices), swap(part_b, bit_b, devices)
        part_a = jnp.concatenate([part_a, got_a], axis=0)
        part_b = jnp.concatenate([part_b, got_b], axis=0)
    part_b = reorder(part_b, places_of(order_b), places_of(order_a), height)
    low_a, low_b = swap(part_a, bits[-1], devices), swap(part_b, bits[-1], devices)

    hidden, weight = hidden_call(own, (part_a, part_b), (low_a, low_b), gate_proj, up_proj)

    outs = []
    for k in range(2):
        keep, send = down_call(hidden, weight, down_proj, k * width, width)
        for bit in reversed(bits):
            total = keep + swap(send, bit, devices).astype(F32)
            half = total.shape[0] // 2
            if bit == bits[0]:
                break
            keep, send = total[:half], total[half:].astype(BF16)
        outs.append(total.astype(BF16))
    return jnp.concatenate(outs, axis=1)


def solution(mesh):
    placed = (
        P(("group", "expert"), None),
        P(("group", "expert"), None),
        P(("group", "expert"), None),
        P(None, "expert"),
        P(None, "expert"),
        P("expert", None),
    )
    return jax.shard_map(
        shards, mesh=mesh, in_specs=placed, out_specs=P(("group", "expert"), None), check_vma=False
    )
```

time: 180 us -> 83.1 us (0.46)
  the two profiles are of different devices: /device:TPU:15 before, /device:TPU:0 now
where the time goes in v2:
time: 83.1 us; the launch traced here: 82.9 us
  Pallas kernels  30.9 us (37%)
  waiting for transfers between devices  30.5 us (37%)
  starting transfers between devices  18.2 us (22%)
  other arithmetic  1.95 us (2%)
  local copies, waits for them, and re-layouts  1.11 us (1%)
    ppermute x15, waiting for transfers between devices, swap(): return lax.ppermute(value, 'expert', [(i, i ^ bit) for i in range(devices)])  30.5 us
    pallas_call x1, Pallas kernels, hidden_call(): pl.pallas_call(functools.partial(hid_kernel, rows, slots), name='gate_up'...  18.8 us
    ppermute x15, starting transfers between devices, swap(): return lax.ppermute(value, 'expert', [(i, i ^ bit) for i in range(devices)])  18.2 us
    pallas_call x2, Pallas kernels, down_call(): pl.pallas_call(functools.partial(down_kernel, offset, slots), name='down_...  12.2 us
  transfers between devices with their start and end apart: 15, of which 12 were waited for; matrix products, arithmetic and copies ran while one was open for 1% of the time, Pallas kernels for 7%

profile of v2, /device:TPU:0, one launch (start us, length us, event | category | flops | bytes accessed | tf_op | source)
XLA Modules:
  0.0 82.9 jit_solution(4728751197888525516)
XLA Ops:
  0.0 0.8 select_reduce_fusion
  0.8 1.0 %concatenate.25 = bf16[8,7296]{1,0:T(8,128)(2,1)S(1)} concatenate(bf16[8,7168]{1,0:T(8,128)(2,1)} %param.6, bf16[8,16]{1,0:T(8,128)(2,1)S(1)} %get-tuple-element.21, bf16[8,16]{1,0:T(8,128)(2,1)S(1)} %get-tuple-element.20, bf16[8,16]{1,0:T(8,128)(2,1)S(1)} %get-tuple-element.19, bf16[8,80]{1,0:T(8,128)(2,1)S(1)} %broadcast_in_dim.20), dimensions={1} | concatenate | bytes 233472 | tf_op jit(solution)/shard_map/concatenate | solution.py:165
  1.8 4.0 %collective-permute-start = (bf16[8,7296]{1,0:T(8,128)(2,1)S(1)}, bf16[8,7296]{1,0:T(8,128)(2,1)S(1)}, u32[]{:S(2)}, u32[]{:S(2)}) collective-permute-start(bf16[8,7296]{1,0:T(8,128)(2,1)S(1)} %concatenate.25), channel_id=1, source_target_pairs={{0,8},{1,9},{2,10},{3,11},{4,12},{5,13},{6,14},{7,15},{8,0},{9,1},... | collective-permute-start | bytes 350216 | tf_op jit(solution)/shard_map/ppermute | solution.py:18
  5.9 5.7 %collective-permute-done = bf16[8,7296]{1,0:T(8,128)(2,1)S(1)} collective-permute-done((bf16[8,7296]{1,0:T(8,128)(2,1)S(1)}, bf16[8,7296]{1,0:T(8,128)(2,1)S(1)}, u32[]{:S(2)}, u32[]{:S(2)}) %collective-permute-start) | collective-permute-done | bytes 116768 | tf_op jit(solution)/shard_map/ppermute | solution.py:18
  11.6 1.6 %collective-permute-start.4 = (bf16[16,3712]{1,0:T(8,128)(2,1)S(1)}, bf16[16,3712]{1,0:T(8,128)(2,1)S(1)}, u32[]{:S(2)}, u32[]{:S(2)}) collective-permute-start(bf16[16,3712]{1,0:T(8,128)(2,1)S(1)} %pad_maximum_fusion.4), channel_id=1, source_target_pairs={{0,2},{1,3},{2,0},{3,1},{4,6},{5,7},{6,4},{7,5},{8,10},{9,11},{10,... | collective-permute-start | bytes 356360 | tf_op jit(solution)/shard_map/ppermute | solution.py:18
  13.2 0.7 collective-permute-start.1
  13.9 2.5 %collective-permute-done.4 = bf16[16,3712]{1,0:T(8,128)(2,1)S(1)} collective-permute-done((bf16[16,3712]{1,0:T(8,128)(2,1)S(1)}, bf16[16,3712]{1,0:T(8,128)(2,1)S(1)}, u32[]{:S(2)}, u32[]{:S(2)}) %collective-permute-start.4) | collective-permute-done | bytes 118816 | tf_op jit(solution)/shard_map/ppermute | solution.py:18
  16.5 1.1 %collective-permute-start.5 = (bf16[32,3712]{1,0:T(8,128)(2,1)S(1)}, bf16[32,3712]{1,0:T(8,128)(2,1)S(1)}, u32[]{:S(2)}, u32[]{:S(2)}) collective-permute-start(bf16[32,3712]{1,0:T(8,128)(2,1)S(1)} %pad_maximum_fusion.2), channel_id=1, source_target_pairs={{0,4},{1,5},{2,6},{3,7},{4,0},{5,1},{6,2},{7,3},{8,12},{9,13},{10,... | collective-permute-start | bytes 712712 | tf_op jit(solution)/shard_map/ppermute | solution.py:18
  17.6 0.9 %collective-permute-done.1 = bf16[16,3584]{1,0:T(8,128)(2,1)S(1)} collective-permute-done((bf16[16,3584]{1,0:T(8,128)(2,1)S(1)}, bf16[16,3584]{1,0:T(8,128)(2,1)S(1)}, u32[]{:S(2)}, u32[]{:S(2)}) %collective-permute-start.1) | collective-permute-done | bytes 114720 | tf_op jit(solution)/shard_map/ppermute | solution.py:18
  18.5 0.7 collective-permute-start.2
  19.2 4.0 %collective-permute-done.5 = bf16[32,3712]{1,0:T(8,128)(2,1)S(1)} collective-permute-done((bf16[32,3712]{1,0:T(8,128)(2,1)S(1)}, bf16[32,3712]{1,0:T(8,128)(2,1)S(1)}, u32[]{:S(2)}, u32[]{:S(2)}) %collective-permute-start.5) | collective-permute-done | bytes 237600 | tf_op jit(solution)/shard_map/ppermute | solution.py:18
  23.2 0.1 pad_maximum_fusion.b0_ref
  23.2 0.1 collective-permute-start.6
  23.3 1.3 %collective-permute-done.2 = bf16[32,3584]{1,0:T(8,128)(2,1)S(1)} collective-permute-done((bf16[32,3584]{1,0:T(8,128)(2,1)S(1)}, bf16[32,3584]{1,0:T(8,128)(2,1)S(1)}, u32[]{:S(2)}, u32[]{:S(2)}) %collective-permute-start.2) | collective-permute-done | bytes 229408 | tf_op jit(solution)/shard_map/ppermute | solution.py:18
  24.6 0.1 collective-permute-start.3
  24.7 1.8 %collective-permute-done.3.a1_ref = bf16[64,3584]{1,0:T(8,128)(2,1)S(1)} collective-permute-done((bf16[64,3584]{1,0:T(8,128)(2,1)S(1)}, bf16[64,3584]{1,0:T(8,128)(2,1)S(1)}, u32[]{:S(2)}, u32[]{:S(2)}) %collective-permute-start.3) | collective-permute-done | bytes 458784 | tf_op jit(solution)/shard_map/ppermute | solution.py:18
  26.5 0.0 collective-permute-done.6.b1_ref
  26.5 18.8 %gate_up.1 = (bf16[128,2048]{1,0:T(8,128)(2,1)S(1)}, f32[128,128]{1,0:T(8,128)S(1)}) custom-call(s32[1]{0:T(128)} %bitcast.own_ref, bf16[64,3584]{1,0:T(8,128)(2,1)S(1)} %pad_maximum_fusion.1.a0_ref, bf16[64,3584]{1,0:T(8,128)(2,1)S(1)} %collective-permute-done.3.a1_ref, bf16[64,3712]{1,0:T(8,128)(2,1)S(1)} %pad_maximum_fusion.b0_ref, ...), custom_call_target="tpu_custom_call" | custom-call | flops 7516192768 | bytes 58720256 | tf_op jit(solution)/shard_map/gate_up/pallas_call | solution.py:93
  45.3 6.1 %down_3584.1 = (f32[64,3584]{1,0:T(8,128)S(1)}, bf16[64,3584]{1,0:T(8,128)(2,1)S(1)}) custom-call(bf16[128,2048]{1,0:T(8,128)(2,1)S(1)} %get-tuple-element.11.h_ref, f32[128,128]{1,0:T(8,128)S(1)} %get-tuple-element.12.w_ref, bf16[2048,7168]{1,0:T(8,128)(2,1)} %d_hbm.3), custom_call_target="tpu_custom_call" | custom-call | flops 1879048192 | bytes 14680064 | tf_op jit(solution)/shard_map/down_3584/pallas_call | solution.py:139
  51.4 0.2 collective-permute-start.11
  51.6 6.1 %down_0.1 = (f32[64,3584]{1,0:T(8,128)S(1)}, bf16[64,3584]{1,0:T(8,128)(2,1)S(1)}) custom-call(bf16[128,2048]{1,0:T(8,128)(2,1)S(1)} %get-tuple-element.11.h_ref, f32[128,128]{1,0:T(8,128)S(1)} %get-tuple-element.12.w_ref, bf16[2048,7168]{1,0:T(8,128)(2,1)} %d_hbm.3), custom_call_target="tpu_custom_call" | custom-call | flops 1879048192 | bytes 14680064 | tf_op jit(solution)/shard_map/down_0/pallas_call | solution.py:139
  57.7 0.4 collective-permute-start.7
  58.1 0.0 collective-permute-done.11
  58.1 0.1 convert_add_fusion
  58.2 1.0 %collective-permute-start.12 = (bf16[32,3584]{1,0:T(8,128)(2,1)S(1)}, bf16[32,3584]{1,0:T(8,128)(2,1)S(1)}, u32[]{:S(2)}, u32[]{:S(2)}) collective-permute-start(bf16[32,3584]{1,0:T(8,128)(2,1)S(1)} %slice.100), channel_id=1, source_target_pairs={{0,2},{1,3},{2,0},{3,1},{4,6},{5,7},{6,4},{7,5},{8,10},{9,11},{10,... | collective-permute-start | bytes 688136 | tf_op jit(solution)/shard_map/ppermute | solution.py:18
  59.3 0.3 collective-permute-done.7
  59.6 0.1 convert_add_fusion.1
  59.7 1.1 %collective-permute-start.8 = (bf16[32,3584]{1,0:T(8,128)(2,1)S(1)}, bf16[32,3584]{1,0:T(8,128)(2,1)S(1)}, u32[]{:S(2)}, u32[]{:S(2)}) collective-permute-start(bf16[32,3584]{1,0:T(8,128)(2,1)S(1)} %slice.101), channel_id=1, source_target_pairs={{0,2},{1,3},{2,0},{3,1},{4,6},{5,7},{6,4},{7,5},{8,10},{9,11},{10,... | collective-permute-start | bytes 688136 | tf_op jit(solution)/shard_map/ppermute | solution.py:18
  60.7 6.0 %collective-permute-done.12 = bf16[32,3584]{1,0:T(8,128)(2,1)S(1)} collective-permute-done((bf16[32,3584]{1,0:T(8,128)(2,1)S(1)}, bf16[32,3584]{1,0:T(8,128)(2,1)S(1)}, u32[]{:S(2)}, u32[]{:S(2)}) %collective-permute-start.12) | collective-permute-done | bytes 229408 | tf_op jit(solution)/shard_map/ppermute | solution.py:18
  66.8 0.7 collective-permute-start.13
  67.5 3.4 %collective-permute-done.8 = bf16[32,3584]{1,0:T(8,128)(2,1)S(1)} collective-permute-done((bf16[32,3584]{1,0:T(8,128)(2,1)S(1)}, bf16[32,3584]{1,0:T(8,128)(2,1)S(1)}, u32[]{:S(2)}, u32[]{:S(2)}) %collective-permute-start.8) | collective-permute-done | bytes 229408 | tf_op jit(solution)/shard_map/ppermute | solution.py:18
  70.9 0.7 collective-permute-start.9
  71.6 0.1 collective-permute-done.13
  71.7 3.4 %collective-permute-start.14 = (bf16[8,3584]{1,0:T(8,128)(2,1)S(1)}, bf16[8,3584]{1,0:T(8,128)(2,1)S(1)}, u32[]{:S(2)}, u32[]{:S(2)}) collective-permute-start(bf16[8,3584]{1,0:T(8,128)(2,1)S(1)} %slice.104), channel_id=1, source_target_pairs={{0,8},{1,9},{2,10},{3,11},{4,12},{5,13},{6,14},{7,15},{8,0},{9,1},... | collective-permute-start | bytes 172040 | tf_op jit(solution)/shard_map/ppermute | solution.py:18
  75.1 1.3 %collective-permute-done.9 = bf16[16,3584]{1,0:T(8,128)(2,1)S(1)} collective-permute-done((bf16[16,3584]{1,0:T(8,128)(2,1)S(1)}, bf16[16,3584]{1,0:T(8,128)(2,1)S(1)}, u32[]{:S(2)}, u32[]{:S(2)}) %collective-permute-start.9) | collective-permute-done | bytes 114720 | tf_op jit(solution)/shard_map/ppermute | solution.py:18
  76.4 2.5 %collective-permute-start.10 = (bf16[8,3584]{1,0:T(8,128)(2,1)S(1)}, bf16[8,3584]{1,0:T(8,128)(2,1)S(1)}, u32[]{:S(2)}, u32[]{:S(2)}) collective-permute-start(bf16[8,3584]{1,0:T(8,128)(2,1)S(1)} %slice.105), channel_id=1, source_target_pairs={{0,8},{1,9},{2,10},{3,11},{4,12},{5,13},{6,14},{7,15},{8,0},{9,1},... | collective-permute-start | bytes 172040 | tf_op jit(solution)/shard_map/ppermute | solution.py:18
  78.9 0.0 collective-permute-done.14
  78.9 3.3 %collective-permute-done.10 = bf16[8,3584]{1,0:T(8,128)(2,1)S(1)} collective-permute-done((bf16[8,3584]{1,0:T(8,128)(2,1)S(1)}, bf16[8,3584]{1,0:T(8,128)(2,1)S(1)}, u32[]{:S(2)}, u32[]{:S(2)}) %collective-permute-start.10) | collective-permute-done | bytes 57376 | tf_op jit(solution)/shard_map/ppermute | solution.py:18
  82.2 0.7 pad_maximum_fusion.6
  (20 shorter events, 0.4 us)
Async XLA Ops:
  1.8 9.7 %collective-permute-start = (bf16[8,7296]{1,0:T(8,128)(2,1)S(1)}, bf16[8,7296]{1,0:T(8,128)(2,1)S(1)}, u32[]{:S(2)}, u32[]{:S(2)}) collective-permute-start(bf16[8,7296]{1,0:T(8,128)(2,1)S(1)} %concatenate.25), channel_id=1, source_target_pairs={{0,8},{1,9},{2,10},{3,11},{4,12},{5,13},{6,14},{7,15},{8,0},{9,1},... | collective-permute-start | bytes 350216 | tf_op jit(solution)/shard_map/ppermute | solution.py:18
  11.6 4.9 %collective-permute-start.4 = (bf16[16,3712]{1,0:T(8,128)(2,1)S(1)}, bf16[16,3712]{1,0:T(8,128)(2,1)S(1)}, u32[]{:S(2)}, u32[]{:S(2)}) collective-permute-start(bf16[16,3712]{1,0:T(8,128)(2,1)S(1)} %pad_maximum_fusion.4), channel_id=1, source_target_pairs={{0,2},{1,3},{2,0},{3,1},{4,6},{5,7},{6,4},{7,5},{8,10},{9,11},{10,... | collective-permute-start | bytes 356360 | tf_op jit(solution)/shard_map/ppermute | solution.py:18
  13.2 5.3 %collective-permute-start.1 = (bf16[16,3584]{1,0:T(8,128)(2,1)S(1)}, bf16[16,3584]{1,0:T(8,128)(2,1)S(1)}, u32[]{:S(2)}, u32[]{:S(2)}) collective-permute-start(bf16[16,3584]{1,0:T(8,128)(2,1)S(1)} %pad_maximum_fusion.5), channel_id=1, source_target_pairs={{0,4},{1,5},{2,6},{3,7},{4,0},{5,1},{6,2},{7,3},{8,12},{9,13},{10,... | collective-permute-start | bytes 344072 | tf_op jit(solution)/shard_map/ppermute | solution.py:18
  16.5 6.6 %collective-permute-start.5 = (bf16[32,3712]{1,0:T(8,128)(2,1)S(1)}, bf16[32,3712]{1,0:T(8,128)(2,1)S(1)}, u32[]{:S(2)}, u32[]{:S(2)}) collective-permute-start(bf16[32,3712]{1,0:T(8,128)(2,1)S(1)} %pad_maximum_fusion.2), channel_id=1, source_target_pairs={{0,4},{1,5},{2,6},{3,7},{4,0},{5,1},{6,2},{7,3},{8,12},{9,13},{10,... | collective-permute-start | bytes 712712 | tf_op jit(solution)/shard_map/ppermute | solution.py:18
  18.5 6.1 %collective-permute-start.2 = (bf16[32,3584]{1,0:T(8,128)(2,1)S(1)}, bf16[32,3584]{1,0:T(8,128)(2,1)S(1)}, u32[]{:S(2)}, u32[]{:S(2)}) collective-permute-start(bf16[32,3584]{1,0:T(8,128)(2,1)S(1)} %pad_maximum_fusion.3), channel_id=1, source_target_pairs={{0,2},{1,3},{2,0},{3,1},{4,6},{5,7},{6,4},{7,5},{8,10},{9,11},{10,... | collective-permute-start | bytes 688136 | tf_op jit(solution)/shard_map/ppermute | solution.py:18
  23.2 3.3 %collective-permute-start.6 = (bf16[64,3712]{1,0:T(8,128)(2,1)S(1)}, bf16[64,3712]{1,0:T(8,128)(2,1)S(1)}, u32[]{:S(2)}, u32[]{:S(2)}) collective-permute-start(bf16[64,3712]{1,0:T(8,128)(2,1)S(1)} %pad_maximum_fusion.b0_ref), channel_id=1, source_target_pairs={{0,1},{1,0},{2,3},{3,2},{4,5},{5,4},{6,7},{7,6},{8,9},{9,8},{10,11... | collective-permute-start | bytes 1425416 | tf_op jit(solution)/shard_map/ppermute | solution.py:18
  24.6 1.9 %collective-permute-start.3 = (bf16[64,3584]{1,0:T(8,128)(2,1)S(1)}, bf16[64,3584]{1,0:T(8,128)(2,1)S(1)}, u32[]{:S(2)}, u32[]{:S(2)}) collective-permute-start(bf16[64,3584]{1,0:T(8,128)(2,1)S(1)} %pad_maximum_fusion.1.a0_ref), channel_id=1, source_target_pairs={{0,1},{1,0},{2,3},{3,2},{4,5},{5,4},{6,7},{7,6},{8,9},{9,8},{10,11... | collective-permute-start | bytes 1376264 | tf_op jit(solution)/shard_map/ppermute | solution.py:18
  51.4 6.7 %collective-permute-start.11 = (bf16[64,3584]{1,0:T(8,128)(2,1)S(1)}, bf16[64,3584]{1,0:T(8,128)(2,1)S(1)}, u32[]{:S(2)}, u32[]{:S(2)}) collective-permute-start(bf16[64,3584]{1,0:T(8,128)(2,1)S(1)} %get-tuple-element.16), channel_id=1, source_target_pairs={{0,1},{1,0},{2,3},{3,2},{4,5},{5,4},{6,7},{7,6},{8,9},{9,8},{10,11... | collective-permute-start | bytes 1376264 | tf_op jit(solution)/shard_map/ppermute | solution.py:18
  57.7 1.9 %collective-permute-start.7 = (bf16[64,3584]{1,0:T(8,128)(2,1)S(1)}, bf16[64,3584]{1,0:T(8,128)(2,1)S(1)}, u32[]{:S(2)}, u32[]{:S(2)}) collective-permute-start(bf16[64,3584]{1,0:T(8,128)(2,1)S(1)} %get-tuple-element.14), channel_id=1, source_target_pairs={{0,1},{1,0},{2,3},{3,2},{4,5},{5,4},{6,7},{7,6},{8,9},{9,8},{10,11... | collective-permute-start | bytes 1376264 | tf_op jit(solution)/shard_map/ppermute | solution.py:18
  58.2 8.5 %collective-permute-start.12 = (bf16[32,3584]{1,0:T(8,128)(2,1)S(1)}, bf16[32,3584]{1,0:T(8,128)(2,1)S(1)}, u32[]{:S(2)}, u32[]{:S(2)}) collective-permute-start(bf16[32,3584]{1,0:T(8,128)(2,1)S(1)} %slice.100), channel_id=1, source_target_pairs={{0,2},{1,3},{2,0},{3,1},{4,6},{5,7},{6,4},{7,5},{8,10},{9,11},{10,... | collective-permute-start | bytes 688136 | tf_op jit(solution)/shard_map/ppermute | solution.py:18
  59.7 11.2 %collective-permute-start.8 = (bf16[32,3584]{1,0:T(8,128)(2,1)S(1)}, bf16[32,3584]{1,0:T(8,128)(2,1)S(1)}, u32[]{:S(2)}, u32[]{:S(2)}) collective-permute-start(bf16[32,3584]{1,0:T(8,128)(2,1)S(1)} %slice.101), channel_id=1, source_target_pairs={{0,2},{1,3},{2,0},{3,1},{4,6},{5,7},{6,4},{7,5},{8,10},{9,11},{10,... | collective-permute-start | bytes 688136 | tf_op jit(solution)/shard_map/ppermute | solution.py:18
  66.8 4.9 %collective-permute-start.13 = (bf16[16,3584]{1,0:T(8,128)(2,1)S(1)}, bf16[16,3584]{1,0:T(8,128)(2,1)S(1)}, u32[]{:S(2)}, u32[]{:S(2)}) collective-permute-start(bf16[16,3584]{1,0:T(8,128)(2,1)S(1)} %slice.102), channel_id=1, source_target_pairs={{0,4},{1,5},{2,6},{3,7},{4,0},{5,1},{6,2},{7,3},{8,12},{9,13},{10,... | collective-permute-start | bytes 344072 | tf_op jit(solution)/shard_map/ppermute | solution.py:18
  70.9 5.5 %collective-permute-start.9 = (bf16[16,3584]{1,0:T(8,128)(2,1)S(1)}, bf16[16,3584]{1,0:T(8,128)(2,1)S(1)}, u32[]{:S(2)}, u32[]{:S(2)}) collective-permute-start(bf16[16,3584]{1,0:T(8,128)(2,1)S(1)} %slice.103), channel_id=1, source_target_pairs={{0,4},{1,5},{2,6},{3,7},{4,0},{5,1},{6,2},{7,3},{8,12},{9,13},{10,... | collective-permute-start | bytes 344072 | tf_op jit(solution)/shard_map/ppermute | solution.py:18
  71.7 7.2 %collective-permute-start.14 = (bf16[8,3584]{1,0:T(8,128)(2,1)S(1)}, bf16[8,3584]{1,0:T(8,128)(2,1)S(1)}, u32[]{:S(2)}, u32[]{:S(2)}) collective-permute-start(bf16[8,3584]{1,0:T(8,128)(2,1)S(1)} %slice.104), channel_id=1, source_target_pairs={{0,8},{1,9},{2,10},{3,11},{4,12},{5,13},{6,14},{7,15},{8,0},{9,1},... | collective-permute-start | bytes 172040 | tf_op jit(solution)/shard_map/ppermute | solution.py:18
  76.4 5.8 %collective-permute-start.10 = (bf16[8,3584]{1,0:T(8,128)(2,1)S(1)}, bf16[8,3584]{1,0:T(8,128)(2,1)S(1)}, u32[]{:S(2)}, u32[]{:S(2)}) collective-permute-start(bf16[8,3584]{1,0:T(8,128)(2,1)S(1)} %slice.105), channel_id=1, source_target_pairs={{0,8},{1,9},{2,10},{3,11},{4,12},{5,13},{6,14},{7,15},{8,0},{9,1},... | collective-permute-start | bytes 172040 | tf_op jit(solution)/shard_map/ppermute | solution.py:18

commit v3 on v0

v3 whole, which is shorter than its diff:
```python
import functools

import jax
import jax.numpy as jnp
from jax import lax
from jax.experimental import pallas as pl
from jax.experimental.pallas import tpu as pltpu
from jax.sharding import PartitionSpec as P

FF = 2048
EXPERTS = 16
EXTRA = 128
F32 = jnp.float32
BF16 = jnp.bfloat16
HELD = 1024
KC = 512
SLOTS = 4
LIMIT = 24


def swap(value, bit, devices):
    return lax.ppermute(value, "expert", [(i, i ^ bit) for i in range(devices)])


def bit_order(devices):
    return [1 << k for k in reversed(range(devices.bit_length() - 1))]


def call(body, name, outs, ins, hbm=0, scratch=(), limit=1, cost=(0, 0, 0)):
    vmem = pl.BlockSpec(memory_space=pltpu.VMEM)
    specs = [vmem] * (len(ins) - hbm) + [pl.BlockSpec(memory_space=pltpu.HBM)] * hbm
    return pl.pallas_call(
        body,
        name=name,
        out_shape=tuple(outs),
        in_specs=specs,
        out_specs=(vmem,) * len(outs),
        scratch_shapes=list(scratch),
        compiler_params=pltpu.CompilerParams(vmem_limit_bytes=limit << 20),
        cost_estimate=pl.CostEstimate(flops=cost[0], transcendentals=cost[1], bytes_accessed=cost[2]),
    )(*ins)


def pack(tokens, expert_ids, gate_probs):
    height, model_width = tokens.shape

    def body(t_ref, i_ref, p_ref, o_ref):
        lane = lax.broadcasted_iota(jnp.int32, (height, EXTRA), 1)
        weight = jnp.zeros((height, EXTRA), F32)
        for k in range(expert_ids.shape[1]):
            weight += jnp.where(lane % EXPERTS == i_ref[:, k : k + 1], p_ref[:, k : k + 1], 0.0)
        high = weight.astype(BF16)
        rest = weight - high.astype(F32)
        middle = rest.astype(BF16)
        last = (rest - middle.astype(F32)).astype(BF16)
        wide = [v.astype(F32) for v in (high, middle, last)]
        extra = jnp.where(lane < EXPERTS, wide[0], jnp.where(lane < 2 * EXPERTS, wide[1], wide[2]))
        o_ref[:, :model_width] = t_ref[...]
        o_ref[:, model_width:] = jnp.where(lane < 3 * EXPERTS, extra, 0.0).astype(BF16)

    shape = jax.ShapeDtypeStruct((height, model_width + EXTRA), BF16)
    return call(body, "pack", [shape], [tokens, expert_ids, gate_probs])[0]


def join(values, outs):
    def body(*refs):
        for ref, (width, blocks) in zip(refs[len(values) :], outs):
            top = 0
            for source, col in blocks:
                block = refs[source][:, col : col + width]
                ref[top : top + block.shape[0], :] = block
                top += block.shape[0]

    shapes = [
        jax.ShapeDtypeStruct((sum(values[k].shape[0] for k, _ in blocks), width), BF16) for width, blocks in outs
    ]
    return call(body, "join", shapes, values, cost=(0, 0, 1 << 18))


def fetch(values, pieces):
    def body(*refs):
        *refs, sems = refs
        count, n = len(values), len(pieces)
        sources, copied, held = refs[count : count + n], refs[count + n : 2 * count + n], refs[2 * count + n :]
        copies = [
            pltpu.make_async_copy(src.at[pl.ds(r, h), pl.ds(c, w)], dst, sems.at[k])
            for k, (src, dst, (_, r, h, c, w)) in enumerate(zip(sources, held, pieces))
        ]
        for copy in copies:
            copy.start()
        for src, dst in zip(refs[:count], copied):
            dst[...] = src[...]
        for copy in copies:
            copy.wait()

    shapes = [jax.ShapeDtypeStruct(v.shape, v.dtype) for v in values]
    shapes += [pltpu.VMEM((h, w), BF16) for _, _, h, _, w in pieces]
    size = sum(2 * h * w for _, _, h, _, w in pieces)
    results = call(
        body,
        "fetch",
        shapes,
        [*values, *[p[0] for p in pieces]],
        hbm=len(pieces),
        scratch=[pltpu.SemaphoreType.DMA((len(pieces),))],
        cost=(0, 0, size),
    )
    return results[: len(values)], results[len(values) :]


def gate_up(own, parts_a, parts_b, blocks_a, blocks_b, held, gate_proj, up_proj, kc, slots, limit):
    model_width, hid = gate_proj.shape
    base = held[0].shape[0] if held else 0
    steps = (model_width - base) // kc
    rows = sum(h for _, _, h in blocks_a)
    split = parts_a[0].shape[1]
    cut = min(hid, 512)

    def body(own_ref, *refs):
        a_refs, refs = refs[: len(parts_a)], refs[len(parts_a) :]
        b_refs, refs = refs[: len(parts_b)], refs[len(parts_b) :]
        held_refs, refs = refs[: len(held)], refs[len(held) :]
        g_hbm, u_hbm, o_ref, w_ref, gbuf, ubuf, gacc, uacc, sems = refs

        def copies(s):
            slot = s % slots
            src = pl.ds(base + s * kc, kc)
            return (
                pltpu.make_async_copy(g_hbm.at[src, :], gbuf.at[slot], sems.at[0, slot]),
                pltpu.make_async_copy(u_hbm.at[src, :], ubuf.at[slot], sems.at[1, slot]),
            )

        for s in range(min(slots, steps)):
            for copy in copies(s):
                copy.start()

        def columns(start, count):
            parts = []
            for lo, hi, group, blocks in ((0, split, a_refs, blocks_a), (split, model_width, b_refs, blocks_b)):
                a, b = max(start, lo) - lo, min(start + count, hi) - lo
                if a < b:
                    parts.append(jnp.concatenate([group[k][r : r + h, a:b] for k, r, h in blocks], axis=0))
            return parts[0] if len(parts) == 1 else jnp.concatenate(parts, axis=1)

        def add(x, weights, acc, first):
            part = jnp.dot(x, weights, preferred_element_type=F32)
            if first:
                acc[...] = part
            else:
                acc[...] += part

        top = 0
        for k, r, h in blocks_b:
            lane = lax.broadcasted_iota(jnp.int32, (h, EXTRA), 1)
            mine = (lane < 3 * EXPERTS) & (lane % EXPERTS == own_ref[0:1, :])
            pieces = jnp.where(mine, b_refs[k][r : r + h, model_width - split :].astype(F32), 0.0)
            w_ref[top : top + h, :] = jnp.broadcast_to(jnp.sum(pieces, axis=1, keepdims=True), (h, EXTRA))
            top += h
        if held:
            x = columns(0, base)
            for ref, acc in zip(held_refs, (gacc, uacc)):
                add(x, ref[...], acc, True)
        for s in range(steps):
            x = columns(base + s * kc, kc)
            for copy, buf, acc in zip(copies(s), (gbuf, ubuf), (gacc, uacc)):
                copy.wait()
                add(x, buf[s % slots], acc, base + s == 0)
            if s + slots < steps:
                for copy in copies(s + slots):
                    copy.start()
        for c in range(0, hid, cut):
            gate = gacc[:, c : c + cut]
            o_ref[:, c : c + cut] = (gate / (1.0 + jnp.exp(-gate)) * uacc[:, c : c + cut]).astype(BF16)

    return call(
        body,
        "gate_up",
        [jax.ShapeDtypeStruct((rows, hid), BF16), jax.ShapeDtypeStruct((rows, EXTRA), F32)],
        [own, *parts_a, *parts_b, *held, gate_proj, up_proj],
        hbm=2,
        scratch=[
            pltpu.VMEM((slots, kc, hid), BF16),
            pltpu.VMEM((slots, kc, hid), BF16),
            pltpu.VMEM((rows, hid), F32),
            pltpu.VMEM((rows, hid), F32),
            pltpu.SemaphoreType.DMA((2, slots)),
        ],
        limit=limit,
        cost=(4 * rows * model_width * hid, rows * hid, 4 * (model_width - base) * hid),
    )


def down(hidden, weight, weights):
    rows, width = hidden.shape[0], weights.shape[1]
    half, nc = rows // 2, 512

    def body(h_ref, w_ref, d_ref, keep_ref, send_ref):
        scale = w_ref[:, 0:1]
        for c in range(0, width, nc):
            part = jnp.dot(h_ref[...], d_ref[:, c : c + nc], preferred_element_type=F32) * scale
            keep_ref[:, c : c + nc] = part[:half]
            send_ref[:, c : c + nc] = part[half:].astype(BF16)

    return call(
        body,
        "down",
        [jax.ShapeDtypeStruct((half, width), F32), jax.ShapeDtypeStruct((half, width), BF16)],
        [hidden, weight, weights],
        limit=6,
        cost=(2 * rows * hidden.shape[1] * width, 0, rows * width),
    )


def add_split(pairs, stay, go):
    width = sum(keep.shape[1] for keep, _ in pairs)
    flat = [value for pair in pairs for value in pair]

    def body(*refs):
        results = refs[len(flat) :]
        col = 0
        for keep_ref, got_ref in zip(refs[0 : len(flat) : 2], refs[1 : len(flat) : 2]):
            wide = keep_ref.shape[1]
            for ref, blocks in zip(results, (stay, go)):
                top = 0
                for r, h in blocks:
                    total = keep_ref[r : r + h, :] + got_ref[r : r + h, :].astype(F32)
                    ref[top : top + h, col : col + wide] = total.astype(ref.dtype)
                    top += h
            col += wide

    shapes = [jax.ShapeDtypeStruct((sum(h for _, h in stay), width), F32 if go else BF16)]
    if go:
        shapes.append(jax.ShapeDtypeStruct((sum(h for _, h in go), width), BF16))
    size = sum(keep.size for keep, _ in pairs)
    return call(body, "add", shapes, flat, limit=2, cost=(size, 0, 2 * size))


def shards(tokens, expert_ids, gate_probs, gate_proj, up_proj, down_proj):
    splits = FF // gate_proj.shape[1]
    height, model_width = tokens.shape
    devices = lax.axis_size("expert")
    place = jnp.full((8, EXTRA), lax.axis_index("expert") // splits, jnp.int32)
    gate_proj, up_proj, down_proj = (
        pltpu.with_memory_space_constraint(w, pltpu.HBM) for w in (gate_proj, up_proj, down_proj)
    )
    hid = gate_proj.shape[1]
    width = model_width // 2
    bits = bit_order(devices)
    far, (bit_a, bit_b), core = bits[:-3], bits[-3:-1], bits[-1]

    rows = pack(tokens, expert_ids, gate_probs)
    wide = rows.shape[1]
    for k, bit in enumerate(far):
        got = swap(rows, bit, devices)
        if k + 1 == len(far):
            (rows, own), (down_a,) = fetch([rows, place], [(down_proj, 0, hid, 0, width)])
            part_a, part_b = join([rows, got], [(width, [(0, 0), (1, 0)]), (wide - width, [(0, width), (1, width)])])
        else:
            (rows,) = join([rows, got], [(wide, [(0, 0), (1, 0)])])
    got_a, got_b = swap(part_a, bit_a, devices), swap(part_b, bit_b, devices)
    (part_a, part_b), held = fetch(
        [part_a, part_b], [(gate_proj, 0, HELD, 0, hid), (up_proj, 0, HELD, 0, hid)]
    )
    part_a, part_b = join(
        [part_a, got_a, part_b, got_b], [(width, [(0, 0), (1, 0)]), (wide - width, [(2, 0), (3, 0)])]
    )
    got_a, got_b = swap(part_a, bit_b, devices), swap(part_b, bit_a, devices)
    (part_a, part_b), (down_b,) = fetch([part_a, part_b], [(down_proj, 0, hid, width, width)])
    low_a, low_b = swap(part_a, core, devices), swap(part_b, core, devices)
    far_a, far_b = swap(got_a, core, devices), swap(got_b, core, devices)
    parts_a, parts_b = [part_a, got_a, low_a, far_a], [part_b, got_b, low_b, far_b]
    size = part_a.shape[0]
    half = size // 2
    blocks_a = [(k, 0, size) for k in range(4)]
    blocks_b = [(k + j, r, half) for k in (0, 2) for r in (0, half) for j in (0, 1)]
    hidden, weight = gate_up(
        own, parts_a, parts_b, blocks_a, blocks_b, held, gate_proj, up_proj, KC, SLOTS, LIMIT
    )

    keep_a, send_a = down(hidden, weight, down_a)
    got_a = swap(send_a, core, devices)
    keep_b, send_b = down(hidden, weight, down_b)
    got_b = swap(send_b, core, devices)
    q = keep_a.shape[0] // 4
    keep_a, send_a = add_split([(keep_a, got_a)], [(0, 2 * q)], [(2 * q, 2 * q)])
    got_a = swap(send_a, bit_b, devices)
    keep_b, send_b = add_split([(keep_b, got_b)], [(0, q), (2 * q, q)], [(q, q), (3 * q, q)])
    got_b = swap(send_b, bit_a, devices)
    keep_a, send_a = add_split([(keep_a, got_a)], [(0, q)], [(q, q)])
    got_a = swap(send_a, bit_a, devices)
    keep_b, send_b = add_split([(keep_b, got_b)], [(0, q)], [(q, q)])
    got_b = swap(send_b, bit_b, devices)
    pairs = [(keep_a, got_a), (keep_b, got_b)]
    for bit in reversed(far):
        q = q // 2
        keep, send = add_split(pairs, [(0, q)], [(q, q)])
        pairs = [(keep, swap(send, bit, devices))]
    return add_split(pairs, [(0, q)], [])[0]


def solution(mesh):
    placed = (
        P(("group", "expert"), None),
        P(("group", "expert"), None),
        P(("group", "expert"), None),
        P(None, "expert"),
        P(None, "expert"),
        P("expert", None),
    )
    return jax.shard_map(
        shards, mesh=mesh, in_specs=placed, out_specs=P(("group", "expert"), None), check_vma=False
    )
```

time: 180 us -> 72.2 us (0.40)
  the two profiles are of different devices: /device:TPU:15 before, /device:TPU:0 now
where the time goes in v3:
time: 72.2 us; the launch traced here: 72 us
  Pallas kernels  35.8 us (50%)
  starting transfers between devices  18.3 us (25%)
  waiting for transfers between devices  15.5 us (21%)
  local copies, waits for them, and re-layouts  2.27 us (3%)
    pallas_call x15, Pallas kernels, call(): pl.pallas_call(body, name=name, out_shape=tuple(outs), in_specs=specs, ou...  35.8 us
    ppermute x16, starting transfers between devices, swap(): return lax.ppermute(value, 'expert', [(i, i ^ bit) for i in range(devices)])  18.3 us
    ppermute x16, waiting for transfers between devices, swap(): return lax.ppermute(value, 'expert', [(i, i ^ bit) for i in range(devices)])  15.5 us
    unnamed x6, local copies, waits for them, and re-layouts  2.27 us
  transfers between devices with their start and end apart: 16, of which 9 were waited for; matrix products, arithmetic and copies ran while one was open for 0% of the time, Pallas kernels for 22%

profile of v3, /device:TPU:0, one launch (start us, length us, event | category | flops | bytes accessed | tf_op | source)
XLA Modules:
  0.0 72.0 jit_solution(4715564144361521615)
XLA Ops:
  0.0 0.0 copy-start
  0.0 0.9 %copy-done = bf16[8,7168]{1,0:T(8,128)(2,1)S(1)} copy-done((bf16[8,7168]{1,0:T(8,128)(2,1)S(1)}, bf16[8,7168]{1,0:T(8,128)(2,1)}, u32[]{:S(2)}) %copy-start) | copy-done | bytes 114712
  0.9 0.0 copy-start.1
  0.9 0.7 copy-done.1
  1.6 0.0 copy-start.2
  1.6 0.7 copy-done.2
  2.3 0.1 pack.1.refs_0_
  2.4 4.1 %collective-permute-start = (bf16[8,7296]{1,0:T(8,128)(2,1)S(1)}, bf16[8,7296]{1,0:T(8,128)(2,1)S(1)}, u32[]{:S(2)}, u32[]{:S(2)}) collective-permute-start(bf16[8,7296]{1,0:T(8,128)(2,1)S(1)} %pack.1.refs_0_), channel_id=1, source_target_pairs={{0,8},{1,9},{2,10},{3,11},{4,12},{5,13},{6,14},{7,15},{8,0},{9,1},... | collective-permute-start | bytes 350216 | tf_op jit(solution)/shard_map/ppermute | solution.py:22
  6.5 5.2 %fetch.3 = (bf16[8,7296]{1,0:T(8,128)(2,1)S(1)}, s32[8,128]{1,0:T(8,128)S(1)}, bf16[2048,3584]{1,0:T(8,128)(2,1)S(1)}) custom-call(bf16[8,7296]{1,0:T(8,128)(2,1)S(1)} %pack.1.refs_0_, s32[8,128]{1,0:T(8,128)S(1)} %broadcast_in_dim.3.refs_1_, bf16[2048,7168]{1,0:T(8,128)(2,1)} %refs_2_.5), custom_call_target="tpu_custom_call" | custom-call | bytes 14680064 | tf_op jit(solution)/shard_map/fetch/pallas_call | solution.py:32
  11.7 0.5 collective-permute-done.refs_1_
  12.2 1.6 %collective-permute-start.2 = (bf16[16,3712]{1,0:T(8,128)(2,1)S(1)}, bf16[16,3712]{1,0:T(8,128)(2,1)S(1)}, u32[]{:S(2)}, u32[]{:S(2)}) collective-permute-start(bf16[16,3712]{1,0:T(8,128)(2,1)S(1)} %get-tuple-element.38.refs_1_), channel_id=1, source_target_pairs={{0,2},{1,3},{2,0},{3,1},{4,6},{5,7},{6,4},{7,5},{8,10},{9,11},{10,... | collective-permute-start | bytes 356360 | tf_op jit(solution)/shard_map/ppermute | solution.py:22
  13.8 1.0 %collective-permute-start.1 = (bf16[16,3584]{1,0:T(8,128)(2,1)S(1)}, bf16[16,3584]{1,0:T(8,128)(2,1)S(1)}, u32[]{:S(2)}, u32[]{:S(2)}) collective-permute-start(bf16[16,3584]{1,0:T(8,128)(2,1)S(1)} %get-tuple-element.37.refs_0_), channel_id=1, source_target_pairs={{0,4},{1,5},{2,6},{3,7},{4,0},{5,1},{6,2},{7,3},{8,12},{9,13},{10,... | collective-permute-start | bytes 344072 | tf_op jit(solution)/shard_map/ppermute | solution.py:22
  14.8 3.5 %fetch.4 = (bf16[16,3584]{1,0:T(8,128)(2,1)S(1)}, bf16[16,3712]{1,0:T(8,128)(2,1)S(1)}, bf16[1024,2048]{1,0:T(8,128)(2,1)S(1)}, bf16[1024,2048]{1,0:T(8,128)(2,1)S(1)}) custom-call(bf16[16,3584]{1,0:T(8,128)(2,1)S(1)} %get-tuple-element.37.refs_0_, bf16[16,3712]{1,0:T(8,128)(2,1)S(1)} %get-tuple-element.38.refs_1_, bf16[7168,2048]{1,0:T(8,128)(2,1)} %refs_10_.1, ...), custom_call_target="tpu_custom_call" | custom-call | bytes 8388608 | tf_op jit(solution)/shard_map/fetch/pallas_call | solution.py:32
  18.3 0.3 collective-permute-done.1.refs_1_
  18.6 0.0 collective-permute-done.2.refs_3_
  18.6 1.1 %collective-permute-start.6 = (bf16[32,3712]{1,0:T(8,128)(2,1)S(1)}, bf16[32,3712]{1,0:T(8,128)(2,1)S(1)}, u32[]{:S(2)}, u32[]{:S(2)}) collective-permute-start(bf16[32,3712]{1,0:T(8,128)(2,1)S(1)} %get-tuple-element.42.refs_1_), channel_id=1, source_target_pairs={{0,4},{1,5},{2,6},{3,7},{4,0},{5,1},{6,2},{7,3},{8,12},{9,13},{10,... | collective-permute-start | bytes 712712 | tf_op jit(solution)/shard_map/ppermute | solution.py:22
  19.7 0.5 collective-permute-start.3
  20.3 5.2 %fetch.5 = (bf16[32,3584]{1,0:T(8,128)(2,1)S(1)}, bf16[32,3712]{1,0:T(8,128)(2,1)S(1)}, bf16[2048,3584]{1,0:T(8,128)(2,1)S(1)}) custom-call(bf16[32,3584]{1,0:T(8,128)(2,1)S(1)} %get-tuple-element.41.refs_0_, bf16[32,3712]{1,0:T(8,128)(2,1)S(1)} %get-tuple-element.42.refs_1_, bf16[2048,7168]{1,0:T(8,128)(2,1)} %refs_2_.5), custom_call_target="tpu_custom_call" | custom-call | bytes 14680064 | tf_op jit(solution)/shard_map/fetch/pallas_call | solution.py:32
  25.5 0.1 collective-permute-start.7
  25.5 0.0 collective-permute-done.6.refs_5_
  25.6 0.5 collective-permute-start.8
  26.0 0.1 collective-permute-start.4
  26.1 0.0 collective-permute-done.3.refs_1_
  26.1 0.4 collective-permute-start.5
  26.6 1.1 %collective-permute-done.4.refs_2_ = bf16[32,3584]{1,0:T(8,128)(2,1)S(1)} collective-permute-done((bf16[32,3584]{1,0:T(8,128)(2,1)S(1)}, bf16[32,3584]{1,0:T(8,128)(2,1)S(1)}, u32[]{:S(2)}, u32[]{:S(2)}) %collective-permute-start.4) | collective-permute-done | bytes 229408 | tf_op jit(solution)/shard_map/ppermute | solution.py:22
  27.7 0.0 collective-permute-done.7.refs_6_
  27.7 0.3 collective-permute-done.5.refs_3_
  28.0 0.0 collective-permute-done.8.refs_7_
  28.0 16.7 %gate_up.1 = (bf16[128,2048]{1,0:T(8,128)(2,1)S(1)}, f32[128,128]{1,0:T(8,128)S(1)}) custom-call(s32[8,128]{1,0:T(8,128)S(1)} %get-tuple-element.35.own_ref, bf16[32,3584]{1,0:T(8,128)(2,1)S(1)} %get-tuple-element.43.refs_0_, bf16[32,3584]{1,0:T(8,128)(2,1)S(1)} %collective-permute-done.3.refs_1_, bf16[32,3584]{1,0:T(8,128)(2,1)S(1)} %collective-permute-done.4.refs_2_, ...), custom_call_target="tpu_custom_call" | custom-call | flops 7516192768 | bytes 50331648 | tf_op jit(solution)/shard_map/gate_up/pallas_call | solution.py:32
  44.8 2.1 %down.3 = (f32[64,3584]{1,0:T(8,128)S(1)}, bf16[64,3584]{1,0:T(8,128)(2,1)S(1)}) custom-call(bf16[128,2048]{1,0:T(8,128)(2,1)S(1)} %get-tuple-element.47.h_ref, f32[128,128]{1,0:T(8,128)S(1)} %get-tuple-element.48.w_ref, bf16[2048,3584]{1,0:T(8,128)(2,1)S(1)} %get-tuple-element.56.d_ref), custom_call_target="tpu_custom_call" | custom-call | flops 1879048192 | bytes 458752 | tf_op jit(solution)/shard_map/down/pallas_call | solution.py:32
  46.8 0.2 collective-permute-start.12
  47.1 2.1 %down.2 = (f32[64,3584]{1,0:T(8,128)S(1)}, bf16[64,3584]{1,0:T(8,128)(2,1)S(1)}) custom-call(bf16[128,2048]{1,0:T(8,128)(2,1)S(1)} %get-tuple-element.47.h_ref, f32[128,128]{1,0:T(8,128)S(1)} %get-tuple-element.48.w_ref, bf16[2048,3584]{1,0:T(8,128)(2,1)S(1)} %get-tuple-element.49.d_ref), custom_call_target="tpu_custom_call" | custom-call | flops 1879048192 | bytes 458752 | tf_op jit(solution)/shard_map/down/pallas_call | solution.py:32
  49.2 0.4 collective-permute-start.9
  49.6 0.0 collective-permute-done.12.refs_1_
  49.6 0.1 add.9
  49.7 1.0 %collective-permute-start.13 = (bf16[32,3584]{1,0:T(8,128)(2,1)S(1)}, bf16[32,3584]{1,0:T(8,128)(2,1)S(1)}, u32[]{:S(2)}, u32[]{:S(2)}) collective-permute-start(bf16[32,3584]{1,0:T(8,128)(2,1)S(1)} %get-tuple-element.60), channel_id=1, source_target_pairs={{0,4},{1,5},{2,6},{3,7},{4,0},{5,1},{6,2},{7,3},{8,12},{9,13},{10,... | collective-permute-start | bytes 688136 | tf_op jit(solution)/shard_map/ppermute | solution.py:22
  50.7 0.4 collective-permute-done.9.refs_1_
  51.1 0.1 add.7
  51.1 1.6 %collective-permute-start.10 = (bf16[32,3584]{1,0:T(8,128)(2,1)S(1)}, bf16[32,3584]{1,0:T(8,128)(2,1)S(1)}, u32[]{:S(2)}, u32[]{:S(2)}) collective-permute-start(bf16[32,3584]{1,0:T(8,128)(2,1)S(1)} %get-tuple-element.53), channel_id=1, source_target_pairs={{0,2},{1,3},{2,0},{3,1},{4,6},{5,7},{6,4},{7,5},{8,10},{9,11},{10,... | collective-permute-start | bytes 688136 | tf_op jit(solution)/shard_map/ppermute | solution.py:22
  52.7 4.7 %collective-permute-done.13.refs_1_ = bf16[32,3584]{1,0:T(8,128)(2,1)S(1)} collective-permute-done((bf16[32,3584]{1,0:T(8,128)(2,1)S(1)}, bf16[32,3584]{1,0:T(8,128)(2,1)S(1)}, u32[]{:S(2)}, u32[]{:S(2)}) %collective-permute-start.13) | collective-permute-done | bytes 229408 | tf_op jit(solution)/shard_map/ppermute | solution.py:22
  57.5 1.6 %collective-permute-start.14 = (bf16[16,3584]{1,0:T(8,128)(2,1)S(1)}, bf16[16,3584]{1,0:T(8,128)(2,1)S(1)}, u32[]{:S(2)}, u32[]{:S(2)}) collective-permute-start(bf16[16,3584]{1,0:T(8,128)(2,1)S(1)} %get-tuple-element.62), channel_id=1, source_target_pairs={{0,2},{1,3},{2,0},{3,1},{4,6},{5,7},{6,4},{7,5},{8,10},{9,11},{10,... | collective-permute-start | bytes 344072 | tf_op jit(solution)/shard_map/ppermute | solution.py:22
  59.0 0.0 collective-permute-done.10.refs_1_
  59.1 1.0 %collective-permute-start.11 = (bf16[16,3584]{1,0:T(8,128)(2,1)S(1)}, bf16[16,3584]{1,0:T(8,128)(2,1)S(1)}, u32[]{:S(2)}, u32[]{:S(2)}) collective-permute-start(bf16[16,3584]{1,0:T(8,128)(2,1)S(1)} %get-tuple-element.55), channel_id=1, source_target_pairs={{0,4},{1,5},{2,6},{3,7},{4,0},{5,1},{6,2},{7,3},{8,12},{9,13},{10,... | collective-permute-start | bytes 344072 | tf_op jit(solution)/shard_map/ppermute | solution.py:22
  60.1 2.2 %collective-permute-done.14.refs_3_ = bf16[16,3584]{1,0:T(8,128)(2,1)S(1)} collective-permute-done((bf16[16,3584]{1,0:T(8,128)(2,1)S(1)}, bf16[16,3584]{1,0:T(8,128)(2,1)S(1)}, u32[]{:S(2)}, u32[]{:S(2)}) %collective-permute-start.14) | collective-permute-done | bytes 114720 | tf_op jit(solution)/shard_map/ppermute | solution.py:22
  62.3 1.6 %collective-permute-done.11.refs_1_ = bf16[16,3584]{1,0:T(8,128)(2,1)S(1)} collective-permute-done((bf16[16,3584]{1,0:T(8,128)(2,1)S(1)}, bf16[16,3584]{1,0:T(8,128)(2,1)S(1)}, u32[]{:S(2)}, u32[]{:S(2)}) %collective-permute-start.11) | collective-permute-done | bytes 114720 | tf_op jit(solution)/shard_map/ppermute | solution.py:22
  64.0 3.1 %collective-permute-start.15 = (bf16[8,7168]{1,0:T(8,128)(2,1)S(1)}, bf16[8,7168]{1,0:T(8,128)(2,1)S(1)}, u32[]{:S(2)}, u32[]{:S(2)}) collective-permute-start(bf16[8,7168]{1,0:T(8,128)(2,1)S(1)} %get-tuple-element.64), channel_id=1, source_target_pairs={{0,8},{1,9},{2,10},{3,11},{4,12},{5,13},{6,14},{7,15},{8,0},{9,1},... | collective-permute-start | bytes 344072 | tf_op jit(solution)/shard_map/ppermute | solution.py:22
  67.1 4.2 %collective-permute-done.15.refs_1_ = bf16[8,7168]{1,0:T(8,128)(2,1)S(1)} collective-permute-done((bf16[8,7168]{1,0:T(8,128)(2,1)S(1)}, bf16[8,7168]{1,0:T(8,128)(2,1)S(1)}, u32[]{:S(2)}, u32[]{:S(2)}) %collective-permute-start.15) | collective-permute-done | bytes 114720 | tf_op jit(solution)/shard_map/ppermute | solution.py:22
  71.3 0.7 add.12
  (6 shorter events, 0.2 us)
Async XLA Ops:
  0.0 0.9 %copy-start = (bf16[8,7168]{1,0:T(8,128)(2,1)S(1)}, bf16[8,7168]{1,0:T(8,128)(2,1)}, u32[]{:S(2)}) copy-start(bf16[8,7168]{1,0:T(8,128)(2,1)} %t_ref.1) | copy-start | bytes 344068
  0.9 0.7 copy-start.1
  1.6 0.7 copy-start.2
  2.4 9.8 %collective-permute-start = (bf16[8,7296]{1,0:T(8,128)(2,1)S(1)}, bf16[8,7296]{1,0:T(8,128)(2,1)S(1)}, u32[]{:S(2)}, u32[]{:S(2)}) collective-permute-start(bf16[8,7296]{1,0:T(8,128)(2,1)S(1)} %pack.1.refs_0_), channel_id=1, source_target_pairs={{0,8},{1,9},{2,10},{3,11},{4,12},{5,13},{6,14},{7,15},{8,0},{9,1},... | collective-permute-start | bytes 350216 | tf_op jit(solution)/shard_map/ppermute | solution.py:22
  12.2 6.4 %collective-permute-start.2 = (bf16[16,3712]{1,0:T(8,128)(2,1)S(1)}, bf16[16,3712]{1,0:T(8,128)(2,1)S(1)}, u32[]{:S(2)}, u32[]{:S(2)}) collective-permute-start(bf16[16,3712]{1,0:T(8,128)(2,1)S(1)} %get-tuple-element.38.refs_1_), channel_id=1, source_target_pairs={{0,2},{1,3},{2,0},{3,1},{4,6},{5,7},{6,4},{7,5},{8,10},{9,11},{10,... | collective-permute-start | bytes 356360 | tf_op jit(solution)/shard_map/ppermute | solution.py:22
  13.8 4.8 %collective-permute-start.1 = (bf16[16,3584]{1,0:T(8,128)(2,1)S(1)}, bf16[16,3584]{1,0:T(8,128)(2,1)S(1)}, u32[]{:S(2)}, u32[]{:S(2)}) collective-permute-start(bf16[16,3584]{1,0:T(8,128)(2,1)S(1)} %get-tuple-element.37.refs_0_), channel_id=1, source_target_pairs={{0,4},{1,5},{2,6},{3,7},{4,0},{5,1},{6,2},{7,3},{8,12},{9,13},{10,... | collective-permute-start | bytes 344072 | tf_op jit(solution)/shard_map/ppermute | solution.py:22
  18.6 6.9 %collective-permute-start.6 = (bf16[32,3712]{1,0:T(8,128)(2,1)S(1)}, bf16[32,3712]{1,0:T(8,128)(2,1)S(1)}, u32[]{:S(2)}, u32[]{:S(2)}) collective-permute-start(bf16[32,3712]{1,0:T(8,128)(2,1)S(1)} %get-tuple-element.42.refs_1_), channel_id=1, source_target_pairs={{0,4},{1,5},{2,6},{3,7},{4,0},{5,1},{6,2},{7,3},{8,12},{9,13},{10,... | collective-permute-start | bytes 712712 | tf_op jit(solution)/shard_map/ppermute | solution.py:22
  19.7 6.4 %collective-permute-start.3 = (bf16[32,3584]{1,0:T(8,128)(2,1)S(1)}, bf16[32,3584]{1,0:T(8,128)(2,1)S(1)}, u32[]{:S(2)}, u32[]{:S(2)}) collective-permute-start(bf16[32,3584]{1,0:T(8,128)(2,1)S(1)} %get-tuple-element.41.refs_0_), channel_id=1, source_target_pairs={{0,2},{1,3},{2,0},{3,1},{4,6},{5,7},{6,4},{7,5},{8,10},{9,11},{10,... | collective-permute-start | bytes 688136 | tf_op jit(solution)/shard_map/ppermute | solution.py:22
  25.5 2.2 %collective-permute-start.7 = (bf16[32,3712]{1,0:T(8,128)(2,1)S(1)}, bf16[32,3712]{1,0:T(8,128)(2,1)S(1)}, u32[]{:S(2)}, u32[]{:S(2)}) collective-permute-start(bf16[32,3712]{1,0:T(8,128)(2,1)S(1)} %get-tuple-element.44.refs_4_), channel_id=1, source_target_pairs={{0,1},{1,0},{2,3},{3,2},{4,5},{5,4},{6,7},{7,6},{8,9},{9,8},{10,11... | collective-permute-start | bytes 712712 | tf_op jit(solution)/shard_map/ppermute | solution.py:22
  25.6 2.5 %collective-permute-start.8 = (bf16[32,3712]{1,0:T(8,128)(2,1)S(1)}, bf16[32,3712]{1,0:T(8,128)(2,1)S(1)}, u32[]{:S(2)}, u32[]{:S(2)}) collective-permute-start(bf16[32,3712]{1,0:T(8,128)(2,1)S(1)} %collective-permute-done.6.refs_5_), channel_id=1, source_target_pairs={{0,1},{1,0},{2,3},{3,2},{4,5},{5,4},{6,7},{7,6},{8,9},{9,8},{10,11... | collective-permute-start | bytes 712712 | tf_op jit(solution)/shard_map/ppermute | solution.py:22
  26.0 1.7 %collective-permute-start.4 = (bf16[32,3584]{1,0:T(8,128)(2,1)S(1)}, bf16[32,3584]{1,0:T(8,128)(2,1)S(1)}, u32[]{:S(2)}, u32[]{:S(2)}) collective-permute-start(bf16[32,3584]{1,0:T(8,128)(2,1)S(1)} %get-tuple-element.43.refs_0_), channel_id=1, source_target_pairs={{0,1},{1,0},{2,3},{3,2},{4,5},{5,4},{6,7},{7,6},{8,9},{9,8},{10,11... | collective-permute-start | bytes 688136 | tf_op jit(solution)/shard_map/ppermute | solution.py:22
  26.1 1.9 %collective-permute-start.5 = (bf16[32,3584]{1,0:T(8,128)(2,1)S(1)}, bf16[32,3584]{1,0:T(8,128)(2,1)S(1)}, u32[]{:S(2)}, u32[]{:S(2)}) collective-permute-start(bf16[32,3584]{1,0:T(8,128)(2,1)S(1)} %collective-permute-done.3.refs_1_), channel_id=1, source_target_pairs={{0,1},{1,0},{2,3},{3,2},{4,5},{5,4},{6,7},{7,6},{8,9},{9,8},{10,11... | collective-permute-start | bytes 688136 | tf_op jit(solution)/shard_map/ppermute | solution.py:22
  46.8 2.7 %collective-permute-start.12 = (bf16[64,3584]{1,0:T(8,128)(2,1)S(1)}, bf16[64,3584]{1,0:T(8,128)(2,1)S(1)}, u32[]{:S(2)}, u32[]{:S(2)}) collective-permute-start(bf16[64,3584]{1,0:T(8,128)(2,1)S(1)} %get-tuple-element.58), channel_id=1, source_target_pairs={{0,1},{1,0},{2,3},{3,2},{4,5},{5,4},{6,7},{7,6},{8,9},{9,8},{10,11... | collective-permute-start | bytes 1376264 | tf_op jit(solution)/shard_map/ppermute | solution.py:22
  49.2 1.9 %collective-permute-start.9 = (bf16[64,3584]{1,0:T(8,128)(2,1)S(1)}, bf16[64,3584]{1,0:T(8,128)(2,1)S(1)}, u32[]{:S(2)}, u32[]{:S(2)}) collective-permute-start(bf16[64,3584]{1,0:T(8,128)(2,1)S(1)} %get-tuple-element.51), channel_id=1, source_target_pairs={{0,1},{1,0},{2,3},{3,2},{4,5},{5,4},{6,7},{7,6},{8,9},{9,8},{10,11... | collective-permute-start | bytes 1376264 | tf_op jit(solution)/shard_map/ppermute | solution.py:22
  49.7 7.8 %collective-permute-start.13 = (bf16[32,3584]{1,0:T(8,128)(2,1)S(1)}, bf16[32,3584]{1,0:T(8,128)(2,1)S(1)}, u32[]{:S(2)}, u32[]{:S(2)}) collective-permute-start(bf16[32,3584]{1,0:T(8,128)(2,1)S(1)} %get-tuple-element.60), channel_id=1, source_target_pairs={{0,4},{1,5},{2,6},{3,7},{4,0},{5,1},{6,2},{7,3},{8,12},{9,13},{10,... | collective-permute-start | bytes 688136 | tf_op jit(solution)/shard_map/ppermute | solution.py:22
  51.1 7.9 %collective-permute-start.10 = (bf16[32,3584]{1,0:T(8,128)(2,1)S(1)}, bf16[32,3584]{1,0:T(8,128)(2,1)S(1)}, u32[]{:S(2)}, u32[]{:S(2)}) collective-permute-start(bf16[32,3584]{1,0:T(8,128)(2,1)S(1)} %get-tuple-element.53), channel_id=1, source_target_pairs={{0,2},{1,3},{2,0},{3,1},{4,6},{5,7},{6,4},{7,5},{8,10},{9,11},{10,... | collective-permute-start | bytes 688136 | tf_op jit(solution)/shard_map/ppermute | solution.py:22
  57.5 4.9 %collective-permute-start.14 = (bf16[16,3584]{1,0:T(8,128)(2,1)S(1)}, bf16[16,3584]{1,0:T(8,128)(2,1)S(1)}, u32[]{:S(2)}, u32[]{:S(2)}) collective-permute-start(bf16[16,3584]{1,0:T(8,128)(2,1)S(1)} %get-tuple-element.62), channel_id=1, source_target_pairs={{0,2},{1,3},{2,0},{3,1},{4,6},{5,7},{6,4},{7,5},{8,10},{9,11},{10,... | collective-permute-start | bytes 344072 | tf_op jit(solution)/shard_map/ppermute | solution.py:22
  59.1 4.9 %collective-permute-start.11 = (bf16[16,3584]{1,0:T(8,128)(2,1)S(1)}, bf16[16,3584]{1,0:T(8,128)(2,1)S(1)}, u32[]{:S(2)}, u32[]{:S(2)}) collective-permute-start(bf16[16,3584]{1,0:T(8,128)(2,1)S(1)} %get-tuple-element.55), channel_id=1, source_target_pairs={{0,4},{1,5},{2,6},{3,7},{4,0},{5,1},{6,2},{7,3},{8,12},{9,13},{10,... | collective-permute-start | bytes 344072 | tf_op jit(solution)/shard_map/ppermute | solution.py:22
  64.0 7.3 %collective-permute-start.15 = (bf16[8,7168]{1,0:T(8,128)(2,1)S(1)}, bf16[8,7168]{1,0:T(8,128)(2,1)S(1)}, u32[]{:S(2)}, u32[]{:S(2)}) collective-permute-start(bf16[8,7168]{1,0:T(8,128)(2,1)S(1)} %get-tuple-element.64), channel_id=1, source_target_pairs={{0,8},{1,9},{2,10},{3,11},{4,12},{5,13},{6,14},{7,15},{8,0},{9,1},... | collective-permute-start | bytes 344072 | tf_op jit(solution)/shard_map/ppermute | solution.py:22

commit v4 on v3

--- a/solution.py
+++ b/solution.py
@@ -12,10 +12,10 @@
 EXTRA = 128
 F32 = jnp.float32
 BF16 = jnp.bfloat16
-HELD = 1024
+HELD = (1024, 512)
 KC = 512
-SLOTS = 4
-LIMIT = 24
+SLOTS = 3
+LIMIT = 17
 
 
 def swap(value, bit, devices):
@@ -41,13 +41,21 @@
     )(*ins)
 
 
-def pack(tokens, expert_ids, gate_probs):
-    height, model_width = tokens.shape
-
-    def body(t_ref, i_ref, p_ref, o_ref):
+def pack(expert_ids, gate_probs):
+    height, top = expert_ids.shape
+
+    def body(i_hbm, p_hbm, o_ref, i_ref, p_ref, sems):
+        copies = [
+            pltpu.make_async_copy(i_hbm, i_ref, sems.at[0]),
+            pltpu.make_async_copy(p_hbm, p_ref, sems.at[1]),
+        ]
+        for copy in copies:
+            copy.start()
+        for copy in copies:
+            copy.wait()
         lane = lax.broadcasted_iota(jnp.int32, (height, EXTRA), 1)
         weight = jnp.zeros((height, EXTRA), F32)
-        for k in range(expert_ids.shape[1]):
+        for k in range(top):
             weight += jnp.where(lane % EXPERTS == i_ref[:, k : k + 1], p_ref[:, k : k + 1], 0.0)
         high = weight.astype(BF16)
         rest = weight - high.astype(F32)
@@ -55,29 +63,46 @@
         last = (rest - middle.astype(F32)).astype(BF16)
         wide = [v.astype(F32) for v in (high, middle, last)]
         extra = jnp.where(lane < EXPERTS, wide[0], jnp.where(lane < 2 * EXPERTS, wide[1], wide[2]))
-        o_ref[:, :model_width] = t_ref[...]
-        o_ref[:, model_width:] = jnp.where(lane < 3 * EXPERTS, extra, 0.0).astype(BF16)
-
-    shape = jax.ShapeDtypeStruct((height, model_width + EXTRA), BF16)
-    return call(body, "pack", [shape], [tokens, expert_ids, gate_probs])[0]
+        o_ref[...] = jnp.where(lane < 3 * EXPERTS, extra, 0.0).astype(BF16)
+
+    return call(
+        body,
+        "pack",
+        [jax.ShapeDtypeStruct((height, EXTRA), BF16)],
+        [expert_ids, gate_probs],
+        hbm=2,
+        scratch=[
+            pltpu.VMEM((height, top), jnp.int32),
+            pltpu.VMEM((height, top), F32),
+            pltpu.SemaphoreType.DMA((2,)),
+        ],
+        cost=(0, 0, 1 << 12),
+    )[0]
 
 
 def join(values, outs):
     def body(*refs):
-        for ref, (width, blocks) in zip(refs[len(values) :], outs):
+        for ref, blocks in zip(refs[len(values) :], outs):
             top = 0
-            for source, col in blocks:
-                block = refs[source][:, col : col + width]
-                ref[top : top + block.shape[0], :] = block
-                top += block.shape[0]
+            for block in blocks:
+                col, height = 0, values[block[0][0]].shape[0]
+                for source, first, width in block:
+                    ref[top : top + height, col : col + width] = refs[source][:, first : first + width]
+                    col += width
+                top += height
 
     shapes = [
-        jax.ShapeDtypeStruct((sum(values[k].shape[0] for k, _ in blocks), width), BF16) for width, blocks in outs
+        jax.ShapeDtypeStruct(
+            (sum(values[block[0][0]].shape[0] for block in blocks), sum(w for _, _, w in blocks[0])), BF16
+        )
+        for blocks in outs
     ]
     return call(body, "join", shapes, values, cost=(0, 0, 1 << 18))
 
 
-def fetch(values, pieces):
+def fetch(values, pieces, brought=()):
+    pieces = [*pieces, *[(v, 0, v.shape[0], 0, v.shape[1]) for v in brought]]
+
     def body(*refs):
         *refs, sems = refs
         count, n = len(values), len(pieces)
@@ -110,11 +135,13 @@
 
 def gate_up(own, parts_a, parts_b, blocks_a, blocks_b, held, gate_proj, up_proj, kc, slots, limit):
     model_width, hid = gate_proj.shape
-    base = held[0].shape[0] if held else 0
-    steps = (model_width - base) // kc
+    sizes = [value.shape[0] for value in held[::2]]
+    base = sum(sizes)
+    steps = [(at, kc) for at in range(base, model_width - kc, kc)]
+    steps += [(at, kc // 2) for at in range(model_width - kc, model_width, kc // 2)]
     rows = sum(h for _, _, h in blocks_a)
     split = parts_a[0].shape[1]
-    cut = min(hid, 512)
+    cut = min(hid, 256)
 
     def body(own_ref, *refs):
         a_refs, refs = refs[: len(parts_a)], refs[len(parts_a) :]
@@ -123,14 +150,14 @@
         g_hbm, u_hbm, o_ref, w_ref, gbuf, ubuf, gacc, uacc, sems = refs
 
         def copies(s):
-            slot = s % slots
-            src = pl.ds(base + s * kc, kc)
+            slot, (at, size) = s % slots, steps[s]
+            src, dst = pl.ds(at, size), pl.ds(0, size)
             return (
-                pltpu.make_async_copy(g_hbm.at[src, :], gbuf.at[slot], sems.at[0, slot]),
-                pltpu.make_async_copy(u_hbm.at[src, :], ubuf.at[slot], sems.at[1, slot]),
+                pltpu.make_async_copy(g_hbm.at[src, :], gbuf.at[slot, dst], sems.at[0, slot]),
+                pltpu.make_async_copy(u_hbm.at[src, :], ubuf.at[slot, dst], sems.at[1, slot]),
             )
 
-        for s in range(min(slots, steps)):
+        for s in range(min(slots, len(steps))):
             for copy in copies(s):
                 copy.start()
 
@@ -156,21 +183,30 @@
             pieces = jnp.where(mine, b_refs[k][r : r + h, model_width - split :].astype(F32), 0.0)
             w_ref[top : top + h, :] = jnp.broadcast_to(jnp.sum(pieces, axis=1, keepdims=True), (h, EXTRA))
             top += h
-        if held:
-            x = columns(0, base)
-            for ref, acc in zip(held_refs, (gacc, uacc)):
-                add(x, ref[...], acc, True)
-        for s in range(steps):
-            x = columns(base + s * kc, kc)
+        at = 0
+        for k, size in enumerate(sizes):
+            x = columns(at, size)
+            for ref, acc in zip(held_refs[2 * k : 2 * k + 2], (gacc, uacc)):
+                add(x, ref[...], acc, at == 0)
+            at += size
+        for s, (at, size) in enumerate(steps[:-1]):
+            x = columns(at, size)
             for copy, buf, acc in zip(copies(s), (gbuf, ubuf), (gacc, uacc)):
                 copy.wait()
-                add(x, buf[s % slots], acc, base + s == 0)
-            if s + slots < steps:
+                add(x, buf[s % slots, :size], acc, at == 0)
+            if s + slots < len(steps):
                 for copy in copies(s + slots):
                     copy.start()
+        at, size = steps[-1]
+        slot = (len(steps) - 1) % slots
+        x = columns(at, size)
+        for copy in copies(len(steps) - 1):
+            copy.wait()
         for c in range(0, hid, cut):
-            gate = gacc[:, c : c + cut]
-            o_ref[:, c : c + cut] = (gate / (1.0 + jnp.exp(-gate)) * uacc[:, c : c + cut]).astype(BF16)
+            cols = slice(c, c + cut)
+            gate = gacc[:, cols] + jnp.dot(x, gbuf[slot, :size, cols], preferred_element_type=F32)
+            up = uacc[:, cols] + jnp.dot(x, ubuf[slot, :size, cols], preferred_element_type=F32)
+            o_ref[:, cols] = (gate / (1.0 + jnp.exp(-gate)) * up).astype(BF16)
 
     return call(
         body,
@@ -240,41 +276,62 @@
     height, model_width = tokens.shape
     devices = lax.axis_size("expert")
     place = jnp.full((8, EXTRA), lax.axis_index("expert") // splits, jnp.int32)
-    gate_proj, up_proj, down_proj = (
-        pltpu.with_memory_space_constraint(w, pltpu.HBM) for w in (gate_proj, up_proj, down_proj)
+    expert_ids, gate_probs, gate_proj, up_proj, down_proj = (
+        pltpu.with_memory_space_constraint(v, pltpu.HBM)
+        for v in (expert_ids, gate_probs, gate_proj, up_proj, down_proj)
     )
     hid = gate_proj.shape[1]
     width = model_width // 2
     bits = bit_order(devices)
     far, (bit_a, bit_b), core = bits[:-3], bits[-3:-1], bits[-1]
 
-    rows = pack(tokens, expert_ids, gate_probs)
-    wide = rows.shape[1]
+    rows = tokens
     for k, bit in enumerate(far):
         got = swap(rows, bit, devices)
+        if k == 0:
+            extra = pack(expert_ids, gate_probs)
+        got_extra = swap(extra, bit, devices)
         if k + 1 == len(far):
-            (rows, own), (down_a,) = fetch([rows, place], [(down_proj, 0, hid, 0, width)])
-            part_a, part_b = join([rows, got], [(width, [(0, 0), (1, 0)]), (wide - width, [(0, width), (1, width)])])
+            first = [pltpu.with_memory_space_constraint(rows, pltpu.HBM)] if k == 0 else []
+            values, (down_a, *brought) = fetch(
+                [extra, place] if first else [extra, place, rows], [(down_proj, 0, hid, 0, width)], first
+            )
+            extra, place, rows = [*values, *brought]
+            part_a, part_b = join(
+                [rows, extra, got, got_extra],
+                [
+                    [[(0, 0, width)], [(2, 0, width)]],
+                    [[(0, width, width), (1, 0, EXTRA)], [(2, width, width), (3, 0, EXTRA)]],
+                ],
+            )
         else:
-            (rows,) = join([rows, got], [(wide, [(0, 0), (1, 0)])])
+            rows, extra = join(
+                [rows, extra, got, got_extra],
+                [[[(0, 0, model_width)], [(2, 0, model_width)]], [[(1, 0, EXTRA)], [(3, 0, EXTRA)]]],
+            )
     got_a, got_b = swap(part_a, bit_a, devices), swap(part_b, bit_b, devices)
     (part_a, part_b), held = fetch(
-        [part_a, part_b], [(gate_proj, 0, HELD, 0, hid), (up_proj, 0, HELD, 0, hid)]
+        [part_a, part_b], [(gate_proj, 0, HELD[0], 0, hid), (up_proj, 0, HELD[0], 0, hid)]
     )
     part_a, part_b = join(
-        [part_a, got_a, part_b, got_b], [(width, [(0, 0), (1, 0)]), (wide - width, [(2, 0), (3, 0)])]
+        [part_a, got_a, part_b, got_b],
+        [[[(0, 0, width)], [(1, 0, width)]], [[(2, 0, width + EXTRA)], [(3, 0, width + EXTRA)]]],
     )
     got_a, got_b = swap(part_a, bit_b, devices), swap(part_b, bit_a, devices)
     (part_a, part_b), (down_b,) = fetch([part_a, part_b], [(down_proj, 0, hid, width, width)])
     low_a, low_b = swap(part_a, core, devices), swap(part_b, core, devices)
     far_a, far_b = swap(got_a, core, devices), swap(got_b, core, devices)
+    (got_a, got_b), more = fetch(
+        [got_a, got_b], [(gate_proj, HELD[0], HELD[1], 0, hid), (up_proj, HELD[0], HELD[1], 0, hid)]
+    )
+    held = [*held, *more]
     parts_a, parts_b = [part_a, got_a, low_a, far_a], [part_b, got_b, low_b, far_b]
     size = part_a.shape[0]
     half = size // 2
     blocks_a = [(k, 0, size) for k in range(4)]
     blocks_b = [(k + j, r, half) for k in (0, 2) for r in (0, half) for j in (0, 1)]
     hidden, weight = gate_up(
-        own, parts_a, parts_b, blocks_a, blocks_b, held, gate_proj, up_proj, KC, SLOTS, LIMIT
+        place, parts_a, parts_b, blocks_a, blocks_b, held, gate_proj, up_proj, KC, SLOTS, LIMIT
     )
 
     keep_a, send_a = down(hidden, weight, down_a)
@@ -290,12 +347,13 @@
     got_a = swap(send_a, bit_a, devices)
     keep_b, send_b = add_split([(keep_b, got_b)], [(0, q)], [(q, q)])
     got_b = swap(send_b, bit_b, devices)
-    pairs = [(keep_a, got_a), (keep_b, got_b)]
     for bit in reversed(far):
         q = q // 2
-        keep, send = add_split(pairs, [(0, q)], [(q, q)])
-        pairs = [(keep, swap(send, bit, devices))]
-    return add_split(pairs, [(0, q)], [])[0]
+        keep_a, send_a = add_split([(keep_a, got_a)], [(0, q)], [(q, q)])
+        got_a = swap(send_a, bit, devices)
+        keep_b, send_b = add_split([(keep_b, got_b)], [(0, q)], [(q, q)])
+        got_b = swap(send_b, bit, devices)
+    return add_split([(keep_a, got_a), (keep_b, got_b)], [(0, q)], [])[0]
 
 
 def solution(mesh):

time: 72.2 us -> 70 us (0.970)
  waiting for transfers between devices: 15.5 us -> 11.3 us
  starting transfers between devices: 18.3 us -> 20.7 us
  local copies, waits for them, and re-layouts: 2.27 us -> 0.01 us
  Pallas kernels: 35.8 us -> 37.6 us
    ppermute x16 -> x18, waiting for transfers between devices: 15.5 us -> 11.3 us  [swap(): return lax.ppermute(value, 'expert', [(i, i ^ bit) for i in range(devices)])]
    ppermute x16 -> x18, starting transfers between devices: 18.3 us -> 20.7 us  [swap(): return lax.ppermute(value, 'expert', [(i, i ^ bit) for i in range(devices)])]
    unnamed x6 -> x0, local copies, waits for them, and re-layouts: 2.27 us -> none
    pallas_call x15 -> x17, Pallas kernels: 35.8 us -> 37.6 us  [call(): pl.pallas_call(body, name=name, out_shape=tuple(outs), in_specs=specs, ou...]
  transfers between devices with their start and end apart: 16 -> 18, of which waited for: 9 -> 6; matrix products, arithmetic and copies ran while one was open for 0% -> 0% of each run, Pallas kernels for 22% -> 28%
where the time goes in v4:
time: 70 us; the launch traced here: 69.8 us
  Pallas kernels  37.6 us (54%)
  starting transfers between devices  20.7 us (30%)
  waiting for transfers between devices  11.3 us (16%)
    pallas_call x17, Pallas kernels, call(): pl.pallas_call(body, name=name, out_shape=tuple(outs), in_specs=specs, ou...  37.6 us
    ppermute x18, starting transfers between devices, swap(): return lax.ppermute(value, 'expert', [(i, i ^ bit) for i in range(devices)])  20.7 us
    ppermute x18, waiting for transfers between devices, swap(): return lax.ppermute(value, 'expert', [(i, i ^ bit) for i in range(devices)])  11.3 us
  transfers between devices with their start and end apart: 18, of which 6 were waited for; matrix products, arithmetic and copies ran while one was open for 0% of the time, Pallas kernels for 28%

profile of v4, /device:TPU:0, one launch (start us, length us, event | category | flops | bytes accessed | tf_op | source)
XLA Modules:
  0.0 69.8 jit_solution(3788237463199368027)
XLA Ops:
  0.0 4.0 %collective-permute-start = (bf16[8,7168]{1,0:T(8,128)(2,1)}, bf16[8,7168]{1,0:T(8,128)(2,1)S(1)}, u32[]{:S(2)}, u32[]{:S(2)}) collective-permute-start(bf16[8,7168]{1,0:T(8,128)(2,1)} %refs_3_.3), channel_id=1, source_target_pairs={{0,8},{1,9},{2,10},{3,11},{4,12},{5,13},{6,14},{7,15},{8,0},{9,1},... | collective-permute-start | bytes 344072 | tf_op jit(solution)/shard_map/ppermute | solution.py:22
  4.0 0.8 %pack.1.refs_0_ = bf16[8,128]{1,0:T(8,128)(2,1)S(1)} custom-call(s32[8,8]{1,0:T(8,128)} %i_hbm.1, f32[8,8]{1,0:T(8,128)} %p_hbm.1), custom_call_target="tpu_custom_call" | custom-call | bytes 4096 | tf_op jit(solution)/shard_map/pack/pallas_call | solution.py:32
  4.9 0.1 collective-permute-start.1
  5.0 5.2 %fetch.4 = (bf16[8,128]{1,0:T(8,128)(2,1)S(1)}, s32[8,128]{1,0:T(8,128)S(1)}, bf16[2048,3584]{1,0:T(8,128)(2,1)S(1)}, bf16[8,7168]{1,0:T(8,128)(2,1)S(1)}) custom-call(bf16[8,128]{1,0:T(8,128)(2,1)S(1)} %pack.1.refs_0_, s32[8,128]{1,0:T(8,128)S(1)} %broadcast_in_dim.3.refs_1_, bf16[2048,7168]{1,0:T(8,128)(2,1)} %refs_2_.6, bf16[8,7168]{1,0:T(8,128)(2,1)} %refs_3_.3), custom_call_target="tpu_custom_call" | custom-call | bytes 14794752 | tf_op jit(solution)/shard_map/fetch/pallas_call | solution.py:32
  10.2 0.0 collective-permute-done.1.refs_3_
  10.2 0.0 collective-permute-done.refs_2_
  10.2 1.9 %collective-permute-start.3 = (bf16[16,3712]{1,0:T(8,128)(2,1)S(1)}, bf16[16,3712]{1,0:T(8,128)(2,1)S(1)}, u32[]{:S(2)}, u32[]{:S(2)}) collective-permute-start(bf16[16,3712]{1,0:T(8,128)(2,1)S(1)} %get-tuple-element.46.refs_1_), channel_id=1, source_target_pairs={{0,2},{1,3},{2,0},{3,1},{4,6},{5,7},{6,4},{7,5},{8,10},{9,11},{10,... | collective-permute-start | bytes 356360 | tf_op jit(solution)/shard_map/ppermute | solution.py:22
  12.1 1.6 %collective-permute-start.2 = (bf16[16,3584]{1,0:T(8,128)(2,1)S(1)}, bf16[16,3584]{1,0:T(8,128)(2,1)S(1)}, u32[]{:S(2)}, u32[]{:S(2)}) collective-permute-start(bf16[16,3584]{1,0:T(8,128)(2,1)S(1)} %get-tuple-element.45.refs_0_), channel_id=1, source_target_pairs={{0,4},{1,5},{2,6},{3,7},{4,0},{5,1},{6,2},{7,3},{8,12},{9,13},{10,... | collective-permute-start | bytes 344072 | tf_op jit(solution)/shard_map/ppermute | solution.py:22
  13.7 3.5 %fetch.5 = (bf16[16,3584]{1,0:T(8,128)(2,1)S(1)}, bf16[16,3712]{1,0:T(8,128)(2,1)S(1)}, bf16[1024,2048]{1,0:T(8,128)(2,1)S(1)}, bf16[1024,2048]{1,0:T(8,128)(2,1)S(1)}) custom-call(bf16[16,3584]{1,0:T(8,128)(2,1)S(1)} %get-tuple-element.45.refs_0_, bf16[16,3712]{1,0:T(8,128)(2,1)S(1)} %get-tuple-element.46.refs_1_, bf16[7168,2048]{1,0:T(8,128)(2,1)} %refs_12_.1, ...), custom_call_target="tpu_custom_call" | custom-call | bytes 8388608 | tf_op jit(solution)/shard_map/fetch/pallas_call | solution.py:32
  17.2 0.0 collective-permute-done.2.refs_1_
  17.2 0.0 collective-permute-done.3.refs_3_
  17.2 1.3 %collective-permute-start.5 = (bf16[32,3712]{1,0:T(8,128)(2,1)S(1)}, bf16[32,3712]{1,0:T(8,128)(2,1)S(1)}, u32[]{:S(2)}, u32[]{:S(2)}) collective-permute-start(bf16[32,3712]{1,0:T(8,128)(2,1)S(1)} %get-tuple-element.50.refs_1_), channel_id=1, source_target_pairs={{0,4},{1,5},{2,6},{3,7},{4,0},{5,1},{6,2},{7,3},{8,12},{9,13},{10,... | collective-permute-start | bytes 712712 | tf_op jit(solution)/shard_map/ppermute | solution.py:22
  18.6 0.5 collective-permute-start.4
  19.1 5.2 %fetch.6 = (bf16[32,3584]{1,0:T(8,128)(2,1)S(1)}, bf16[32,3712]{1,0:T(8,128)(2,1)S(1)}, bf16[2048,3584]{1,0:T(8,128)(2,1)S(1)}) custom-call(bf16[32,3584]{1,0:T(8,128)(2,1)S(1)} %get-tuple-element.49.refs_0_, bf16[32,3712]{1,0:T(8,128)(2,1)S(1)} %get-tuple-element.50.refs_1_, bf16[2048,7168]{1,0:T(8,128)(2,1)} %refs_2_.6), custom_call_target="tpu_custom_call" | custom-call | bytes 14680064 | tf_op jit(solution)/shard_map/fetch/pallas_call | solution.py:32
  24.3 0.1 collective-permute-start.8
  24.4 0.0 collective-permute-done.5.refs_1_
  24.4 0.5 collective-permute-start.9
  24.9 0.1 collective-permute-start.6
  25.0 0.0 collective-permute-done.4.refs_0_
  25.0 0.4 collective-permute-start.7
  25.4 2.2 %fetch.7 = (bf16[32,3584]{1,0:T(8,128)(2,1)S(1)}, bf16[32,3712]{1,0:T(8,128)(2,1)S(1)}, bf16[512,2048]{1,0:T(8,128)(2,1)S(1)}, bf16[512,2048]{1,0:T(8,128)(2,1)S(1)}) custom-call(bf16[32,3584]{1,0:T(8,128)(2,1)S(1)} %collective-permute-done.4.refs_0_, bf16[32,3712]{1,0:T(8,128)(2,1)S(1)} %collective-permute-done.5.refs_1_, bf16[7168,2048]{1,0:T(8,128)(2,1)} %refs_12_.1, ...), custom_call_target="tpu_custom_call" | custom-call | bytes 4194304 | tf_op jit(solution)/shard_map/fetch/pallas_call | solution.py:32
  27.6 0.0 collective-permute-done.6.refs_2_
  27.6 0.0 collective-permute-done.8.refs_6_
  27.7 0.0 collective-permute-done.7.refs_3_
  27.7 0.0 collective-permute-done.9.refs_7_
  27.7 15.5 %gate_up.1 = (bf16[128,2048]{1,0:T(8,128)(2,1)S(1)}, f32[128,128]{1,0:T(8,128)S(1)}) custom-call(s32[8,128]{1,0:T(8,128)S(1)} %get-tuple-element.42.own_ref, bf16[32,3584]{1,0:T(8,128)(2,1)S(1)} %get-tuple-element.51.refs_0_, bf16[32,3584]{1,0:T(8,128)(2,1)S(1)} %get-tuple-element.52.refs_1_, bf16[32,3584]{1,0:T(8,128)(2,1)S(1)} %collective-permute-done.6.refs_2_, ...), custom_call_target="tpu_custom_call" | custom-call | flops 7516192768 | bytes 46137344 | tf_op jit(solution)/shard_map/gate_up/pallas_call | solution.py:32
  43.2 2.1 %down.3 = (f32[64,3584]{1,0:T(8,128)S(1)}, bf16[64,3584]{1,0:T(8,128)(2,1)S(1)}) custom-call(bf16[128,2048]{1,0:T(8,128)(2,1)S(1)} %get-tuple-element.59.h_ref, f32[128,128]{1,0:T(8,128)S(1)} %get-tuple-element.60.w_ref, bf16[2048,3584]{1,0:T(8,128)(2,1)S(1)} %get-tuple-element.70.d_ref), custom_call_target="tpu_custom_call" | custom-call | flops 1879048192 | bytes 458752 | tf_op jit(solution)/shard_map/down/pallas_call | solution.py:32
  45.3 0.2 collective-permute-start.14
  45.4 2.1 %down.2 = (f32[64,3584]{1,0:T(8,128)S(1)}, bf16[64,3584]{1,0:T(8,128)(2,1)S(1)}) custom-call(bf16[128,2048]{1,0:T(8,128)(2,1)S(1)} %get-tuple-element.59.h_ref, f32[128,128]{1,0:T(8,128)S(1)} %get-tuple-element.60.w_ref, bf16[2048,3584]{1,0:T(8,128)(2,1)S(1)} %get-tuple-element.61.d_ref), custom_call_target="tpu_custom_call" | custom-call | flops 1879048192 | bytes 458752 | tf_op jit(solution)/shard_map/down/pallas_call | solution.py:32
  47.5 0.5 collective-permute-start.10
  48.0 0.0 collective-permute-done.14.refs_1_
  48.0 0.1 add.11
  48.1 0.8 %collective-permute-start.15 = (bf16[32,3584]{1,0:T(8,128)(2,1)S(1)}, bf16[32,3584]{1,0:T(8,128)(2,1)S(1)}, u32[]{:S(2)}, u32[]{:S(2)}) collective-permute-start(bf16[32,3584]{1,0:T(8,128)(2,1)S(1)} %get-tuple-element.74), channel_id=1, source_target_pairs={{0,4},{1,5},{2,6},{3,7},{4,0},{5,1},{6,2},{7,3},{8,12},{9,13},{10,... | collective-permute-start | bytes 688136 | tf_op jit(solution)/shard_map/ppermute | solution.py:22
  48.9 0.5 collective-permute-done.10.refs_1_
  49.4 0.1 add.8
  49.5 1.6 %collective-permute-start.11 = (bf16[32,3584]{1,0:T(8,128)(2,1)S(1)}, bf16[32,3584]{1,0:T(8,128)(2,1)S(1)}, u32[]{:S(2)}, u32[]{:S(2)}) collective-permute-start(bf16[32,3584]{1,0:T(8,128)(2,1)S(1)} %get-tuple-element.65), channel_id=1, source_target_pairs={{0,2},{1,3},{2,0},{3,1},{4,6},{5,7},{6,4},{7,5},{8,10},{9,11},{10,... | collective-permute-start | bytes 688136 | tf_op jit(solution)/shard_map/ppermute | solution.py:22
  51.1 4.6 %collective-permute-done.15.refs_1_ = bf16[32,3584]{1,0:T(8,128)(2,1)S(1)} collective-permute-done((bf16[32,3584]{1,0:T(8,128)(2,1)S(1)}, bf16[32,3584]{1,0:T(8,128)(2,1)S(1)}, u32[]{:S(2)}, u32[]{:S(2)}) %collective-permute-start.15) | collective-permute-done | bytes 229408 | tf_op jit(solution)/shard_map/ppermute | solution.py:22
  55.8 1.5 %collective-permute-start.16 = (bf16[16,3584]{1,0:T(8,128)(2,1)S(1)}, bf16[16,3584]{1,0:T(8,128)(2,1)S(1)}, u32[]{:S(2)}, u32[]{:S(2)}) collective-permute-start(bf16[16,3584]{1,0:T(8,128)(2,1)S(1)} %get-tuple-element.76), channel_id=1, source_target_pairs={{0,2},{1,3},{2,0},{3,1},{4,6},{5,7},{6,4},{7,5},{8,10},{9,11},{10,... | collective-permute-start | bytes 344072 | tf_op jit(solution)/shard_map/ppermute | solution.py:22
  57.3 0.1 collective-permute-done.11.refs_1_
  57.5 0.8 %collective-permute-start.12 = (bf16[16,3584]{1,0:T(8,128)(2,1)S(1)}, bf16[16,3584]{1,0:T(8,128)(2,1)S(1)}, u32[]{:S(2)}, u32[]{:S(2)}) collective-permute-start(bf16[16,3584]{1,0:T(8,128)(2,1)S(1)} %get-tuple-element.67), channel_id=1, source_target_pairs={{0,4},{1,5},{2,6},{3,7},{4,0},{5,1},{6,2},{7,3},{8,12},{9,13},{10,... | collective-permute-start | bytes 344072 | tf_op jit(solution)/shard_map/ppermute | solution.py:22
  58.3 2.3 %collective-permute-done.16.refs_1_ = bf16[16,3584]{1,0:T(8,128)(2,1)S(1)} collective-permute-done((bf16[16,3584]{1,0:T(8,128)(2,1)S(1)}, bf16[16,3584]{1,0:T(8,128)(2,1)S(1)}, u32[]{:S(2)}, u32[]{:S(2)}) %collective-permute-start.16) | collective-permute-done | bytes 114720 | tf_op jit(solution)/shard_map/ppermute | solution.py:22
  60.7 2.7 %collective-permute-start.17 = (bf16[8,3584]{1,0:T(8,128)(2,1)S(1)}, bf16[8,3584]{1,0:T(8,128)(2,1)S(1)}, u32[]{:S(2)}, u32[]{:S(2)}) collective-permute-start(bf16[8,3584]{1,0:T(8,128)(2,1)S(1)} %get-tuple-element.78), channel_id=1, source_target_pairs={{0,8},{1,9},{2,10},{3,11},{4,12},{5,13},{6,14},{7,15},{8,0},{9,1},... | collective-permute-start | bytes 172040 | tf_op jit(solution)/shard_map/ppermute | solution.py:22
  63.3 0.0 collective-permute-done.12.refs_1_
  63.4 2.1 %collective-permute-start.13 = (bf16[8,3584]{1,0:T(8,128)(2,1)S(1)}, bf16[8,3584]{1,0:T(8,128)(2,1)S(1)}, u32[]{:S(2)}, u32[]{:S(2)}) collective-permute-start(bf16[8,3584]{1,0:T(8,128)(2,1)S(1)} %get-tuple-element.69), channel_id=1, source_target_pairs={{0,8},{1,9},{2,10},{3,11},{4,12},{5,13},{6,14},{7,15},{8,0},{9,1},... | collective-permute-start | bytes 172040 | tf_op jit(solution)/shard_map/ppermute | solution.py:22
  65.5 1.7 %collective-permute-done.17.refs_3_ = bf16[8,3584]{1,0:T(8,128)(2,1)S(1)} collective-permute-done((bf16[8,3584]{1,0:T(8,128)(2,1)S(1)}, bf16[8,3584]{1,0:T(8,128)(2,1)S(1)}, u32[]{:S(2)}, u32[]{:S(2)}) %collective-permute-start.17) | collective-permute-done | bytes 57376 | tf_op jit(solution)/shard_map/ppermute | solution.py:22
  67.2 1.9 %collective-permute-done.13.refs_1_ = bf16[8,3584]{1,0:T(8,128)(2,1)S(1)} collective-permute-done((bf16[8,3584]{1,0:T(8,128)(2,1)S(1)}, bf16[8,3584]{1,0:T(8,128)(2,1)S(1)}, u32[]{:S(2)}, u32[]{:S(2)}) %collective-permute-start.13) | collective-permute-done | bytes 57376 | tf_op jit(solution)/shard_map/ppermute | solution.py:22
  69.1 0.7 add.14
  (7 shorter events, 0.2 us)
Async XLA Ops:
  0.0 10.2 %collective-permute-start = (bf16[8,7168]{1,0:T(8,128)(2,1)}, bf16[8,7168]{1,0:T(8,128)(2,1)S(1)}, u32[]{:S(2)}, u32[]{:S(2)}) collective-permute-start(bf16[8,7168]{1,0:T(8,128)(2,1)} %refs_3_.3), channel_id=1, source_target_pairs={{0,8},{1,9},{2,10},{3,11},{4,12},{5,13},{6,14},{7,15},{8,0},{9,1},... | collective-permute-start | bytes 344072 | tf_op jit(solution)/shard_map/ppermute | solution.py:22
  4.9 5.3 %collective-permute-start.1 = (bf16[8,128]{1,0:T(8,128)(2,1)S(1)}, bf16[8,128]{1,0:T(8,128)(2,1)S(1)}, u32[]{:S(2)}, u32[]{:S(2)}) collective-permute-start(bf16[8,128]{1,0:T(8,128)(2,1)S(1)} %pack.1.refs_0_), channel_id=1, source_target_pairs={{0,8},{1,9},{2,10},{3,11},{4,12},{5,13},{6,14},{7,15},{8,0},{9,1},... | collective-permute-start | bytes 6152 | tf_op jit(solution)/shard_map/ppermute | solution.py:22
  10.2 6.9 %collective-permute-start.3 = (bf16[16,3712]{1,0:T(8,128)(2,1)S(1)}, bf16[16,3712]{1,0:T(8,128)(2,1)S(1)}, u32[]{:S(2)}, u32[]{:S(2)}) collective-permute-start(bf16[16,3712]{1,0:T(8,128)(2,1)S(1)} %get-tuple-element.46.refs_1_), channel_id=1, source_target_pairs={{0,2},{1,3},{2,0},{3,1},{4,6},{5,7},{6,4},{7,5},{8,10},{9,11},{10,... | collective-permute-start | bytes 356360 | tf_op jit(solution)/shard_map/ppermute | solution.py:22
  12.1 5.1 %collective-permute-start.2 = (bf16[16,3584]{1,0:T(8,128)(2,1)S(1)}, bf16[16,3584]{1,0:T(8,128)(2,1)S(1)}, u32[]{:S(2)}, u32[]{:S(2)}) collective-permute-start(bf16[16,3584]{1,0:T(8,128)(2,1)S(1)} %get-tuple-element.45.refs_0_), channel_id=1, source_target_pairs={{0,4},{1,5},{2,6},{3,7},{4,0},{5,1},{6,2},{7,3},{8,12},{9,13},{10,... | collective-permute-start | bytes 344072 | tf_op jit(solution)/shard_map/ppermute | solution.py:22
  17.2 7.2 %collective-permute-start.5 = (bf16[32,3712]{1,0:T(8,128)(2,1)S(1)}, bf16[32,3712]{1,0:T(8,128)(2,1)S(1)}, u32[]{:S(2)}, u32[]{:S(2)}) collective-permute-start(bf16[32,3712]{1,0:T(8,128)(2,1)S(1)} %get-tuple-element.50.refs_1_), channel_id=1, source_target_pairs={{0,4},{1,5},{2,6},{3,7},{4,0},{5,1},{6,2},{7,3},{8,12},{9,13},{10,... | collective-permute-start | bytes 712712 | tf_op jit(solution)/shard_map/ppermute | solution.py:22
  18.6 6.4 %collective-permute-start.4 = (bf16[32,3584]{1,0:T(8,128)(2,1)S(1)}, bf16[32,3584]{1,0:T(8,128)(2,1)S(1)}, u32[]{:S(2)}, u32[]{:S(2)}) collective-permute-start(bf16[32,3584]{1,0:T(8,128)(2,1)S(1)} %get-tuple-element.49.refs_0_), channel_id=1, source_target_pairs={{0,2},{1,3},{2,0},{3,1},{4,6},{5,7},{6,4},{7,5},{8,10},{9,11},{10,... | collective-permute-start | bytes 688136 | tf_op jit(solution)/shard_map/ppermute | solution.py:22
  24.3 3.4 %collective-permute-start.8 = (bf16[32,3712]{1,0:T(8,128)(2,1)S(1)}, bf16[32,3712]{1,0:T(8,128)(2,1)S(1)}, u32[]{:S(2)}, u32[]{:S(2)}) collective-permute-start(bf16[32,3712]{1,0:T(8,128)(2,1)S(1)} %get-tuple-element.53.refs_4_), channel_id=1, source_target_pairs={{0,1},{1,0},{2,3},{3,2},{4,5},{5,4},{6,7},{7,6},{8,9},{9,8},{10,11... | collective-permute-start | bytes 712712 | tf_op jit(solution)/shard_map/ppermute | solution.py:22
  24.4 3.3 %collective-permute-start.9 = (bf16[32,3712]{1,0:T(8,128)(2,1)S(1)}, bf16[32,3712]{1,0:T(8,128)(2,1)S(1)}, u32[]{:S(2)}, u32[]{:S(2)}) collective-permute-start(bf16[32,3712]{1,0:T(8,128)(2,1)S(1)} %collective-permute-done.5.refs_1_), channel_id=1, source_target_pairs={{0,1},{1,0},{2,3},{3,2},{4,5},{5,4},{6,7},{7,6},{8,9},{9,8},{10,11... | collective-permute-start | bytes 712712 | tf_op jit(solution)/shard_map/ppermute | solution.py:22
  24.9 2.8 %collective-permute-start.6 = (bf16[32,3584]{1,0:T(8,128)(2,1)S(1)}, bf16[32,3584]{1,0:T(8,128)(2,1)S(1)}, u32[]{:S(2)}, u32[]{:S(2)}) collective-permute-start(bf16[32,3584]{1,0:T(8,128)(2,1)S(1)} %get-tuple-element.51.refs_0_), channel_id=1, source_target_pairs={{0,1},{1,0},{2,3},{3,2},{4,5},{5,4},{6,7},{7,6},{8,9},{9,8},{10,11... | collective-permute-start | bytes 688136 | tf_op jit(solution)/shard_map/ppermute | solution.py:22
  25.0 2.7 %collective-permute-start.7 = (bf16[32,3584]{1,0:T(8,128)(2,1)S(1)}, bf16[32,3584]{1,0:T(8,128)(2,1)S(1)}, u32[]{:S(2)}, u32[]{:S(2)}) collective-permute-start(bf16[32,3584]{1,0:T(8,128)(2,1)S(1)} %collective-permute-done.4.refs_0_), channel_id=1, source_target_pairs={{0,1},{1,0},{2,3},{3,2},{4,5},{5,4},{6,7},{7,6},{8,9},{9,8},{10,11... | collective-permute-start | bytes 688136 | tf_op jit(solution)/shard_map/ppermute | solution.py:22
  45.3 2.7 %collective-permute-start.14 = (bf16[64,3584]{1,0:T(8,128)(2,1)S(1)}, bf16[64,3584]{1,0:T(8,128)(2,1)S(1)}, u32[]{:S(2)}, u32[]{:S(2)}) collective-permute-start(bf16[64,3584]{1,0:T(8,128)(2,1)S(1)} %get-tuple-element.72), channel_id=1, source_target_pairs={{0,1},{1,0},{2,3},{3,2},{4,5},{5,4},{6,7},{7,6},{8,9},{9,8},{10,11... | collective-permute-start | bytes 1376264 | tf_op jit(solution)/shard_map/ppermute | solution.py:22
  47.5 1.9 %collective-permute-start.10 = (bf16[64,3584]{1,0:T(8,128)(2,1)S(1)}, bf16[64,3584]{1,0:T(8,128)(2,1)S(1)}, u32[]{:S(2)}, u32[]{:S(2)}) collective-permute-start(bf16[64,3584]{1,0:T(8,128)(2,1)S(1)} %get-tuple-element.63), channel_id=1, source_target_pairs={{0,1},{1,0},{2,3},{3,2},{4,5},{5,4},{6,7},{7,6},{8,9},{9,8},{10,11... | collective-permute-start | bytes 1376264 | tf_op jit(solution)/shard_map/ppermute | solution.py:22
  48.1 7.7 %collective-permute-start.15 = (bf16[32,3584]{1,0:T(8,128)(2,1)S(1)}, bf16[32,3584]{1,0:T(8,128)(2,1)S(1)}, u32[]{:S(2)}, u32[]{:S(2)}) collective-permute-start(bf16[32,3584]{1,0:T(8,128)(2,1)S(1)} %get-tuple-element.74), channel_id=1, source_target_pairs={{0,4},{1,5},{2,6},{3,7},{4,0},{5,1},{6,2},{7,3},{8,12},{9,13},{10,... | collective-permute-start | bytes 688136 | tf_op jit(solution)/shard_map/ppermute | solution.py:22
  49.5 7.9 %collective-permute-start.11 = (bf16[32,3584]{1,0:T(8,128)(2,1)S(1)}, bf16[32,3584]{1,0:T(8,128)(2,1)S(1)}, u32[]{:S(2)}, u32[]{:S(2)}) collective-permute-start(bf16[32,3584]{1,0:T(8,128)(2,1)S(1)} %get-tuple-element.65), channel_id=1, source_target_pairs={{0,2},{1,3},{2,0},{3,1},{4,6},{5,7},{6,4},{7,5},{8,10},{9,11},{10,... | collective-permute-start | bytes 688136 | tf_op jit(solution)/shard_map/ppermute | solution.py:22
  55.8 4.9 %collective-permute-start.16 = (bf16[16,3584]{1,0:T(8,128)(2,1)S(1)}, bf16[16,3584]{1,0:T(8,128)(2,1)S(1)}, u32[]{:S(2)}, u32[]{:S(2)}) collective-permute-start(bf16[16,3584]{1,0:T(8,128)(2,1)S(1)} %get-tuple-element.76), channel_id=1, source_target_pairs={{0,2},{1,3},{2,0},{3,1},{4,6},{5,7},{6,4},{7,5},{8,10},{9,11},{10,... | collective-permute-start | bytes 344072 | tf_op jit(solution)/shard_map/ppermute | solution.py:22
  57.5 5.8 %collective-permute-start.12 = (bf16[16,3584]{1,0:T(8,128)(2,1)S(1)}, bf16[16,3584]{1,0:T(8,128)(2,1)S(1)}, u32[]{:S(2)}, u32[]{:S(2)}) collective-permute-start(bf16[16,3584]{1,0:T(8,128)(2,1)S(1)} %get-tuple-element.67), channel_id=1, source_target_pairs={{0,4},{1,5},{2,6},{3,7},{4,0},{5,1},{6,2},{7,3},{8,12},{9,13},{10,... | collective-permute-start | bytes 344072 | tf_op jit(solution)/shard_map/ppermute | solution.py:22
  60.7 6.5 %collective-permute-start.17 = (bf16[8,3584]{1,0:T(8,128)(2,1)S(1)}, bf16[8,3584]{1,0:T(8,128)(2,1)S(1)}, u32[]{:S(2)}, u32[]{:S(2)}) collective-permute-start(bf16[8,3584]{1,0:T(8,128)(2,1)S(1)} %get-tuple-element.78), channel_id=1, source_target_pairs={{0,8},{1,9},{2,10},{3,11},{4,12},{5,13},{6,14},{7,15},{8,0},{9,1},... | collective-permute-start | bytes 172040 | tf_op jit(solution)/shard_map/ppermute | solution.py:22
  63.4 5.8 %collective-permute-start.13 = (bf16[8,3584]{1,0:T(8,128)(2,1)S(1)}, bf16[8,3584]{1,0:T(8,128)(2,1)S(1)}, u32[]{:S(2)}, u32[]{:S(2)}) collective-permute-start(bf16[8,3584]{1,0:T(8,128)(2,1)S(1)} %get-tuple-element.69), channel_id=1, source_target_pairs={{0,8},{1,9},{2,10},{3,11},{4,12},{5,13},{6,14},{7,15},{8,0},{9,1},... | collective-permute-start | bytes 172040 | tf_op jit(solution)/shard_map/ppermute | solution.py:22

commit v5 on v4

--- a/solution.py
+++ b/solution.py
@@ -138,10 +138,10 @@
     sizes = [value.shape[0] for value in held[::2]]
     base = sum(sizes)
     steps = [(at, kc) for at in range(base, model_width - kc, kc)]
-    steps += [(at, kc // 2) for at in range(model_width - kc, model_width, kc // 2)]
+    steps += [(model_width - kc, kc - kc // 4), (model_width - kc // 4, kc // 4)]
     rows = sum(h for _, _, h in blocks_a)
     split = parts_a[0].shape[1]
-    cut = min(hid, 256)
+    cut = min(hid, 512)
 
     def body(own_ref, *refs):
         a_refs, refs = refs[: len(parts_a)], refs[len(parts_a) :]

time: 70 us -> 70 us (level)
  no operation moved by 1% of the time
where the time goes in v5:
time: 70 us; the launch traced here: 69.8 us
  Pallas kernels  37.6 us (54%)
  starting transfers between devices  20.7 us (30%)
  waiting for transfers between devices  11.3 us (16%)
    pallas_call x17, Pallas kernels, call(): pl.pallas_call(body, name=name, out_shape=tuple(outs), in_specs=specs, ou...  37.6 us
    ppermute x18, starting transfers between devices, swap(): return lax.ppermute(value, 'expert', [(i, i ^ bit) for i in range(devices)])  20.7 us
    ppermute x18, waiting for transfers between devices, swap(): return lax.ppermute(value, 'expert', [(i, i ^ bit) for i in range(devices)])  11.3 us
  transfers between devices with their start and end apart: 18, of which 6 were waited for; matrix products, arithmetic and copies ran while one was open for 0% of the time, Pallas kernels for 28%

profile of v5, /device:TPU:0, one launch (start us, length us, event | category | flops | bytes accessed | tf_op | source)
XLA Modules:
  0.0 69.8 jit_solution(9148602583540026847)
XLA Ops:
  0.0 4.0 %collective-permute-start = (bf16[8,7168]{1,0:T(8,128)(2,1)}, bf16[8,7168]{1,0:T(8,128)(2,1)S(1)}, u32[]{:S(2)}, u32[]{:S(2)}) collective-permute-start(bf16[8,7168]{1,0:T(8,128)(2,1)} %refs_3_.3), channel_id=1, source_target_pairs={{0,8},{1,9},{2,10},{3,11},{4,12},{5,13},{6,14},{7,15},{8,0},{9,1},... | collective-permute-start | bytes 344072 | tf_op jit(solution)/shard_map/ppermute | solution.py:22
  4.0 0.8 %pack.1.refs_0_ = bf16[8,128]{1,0:T(8,128)(2,1)S(1)} custom-call(s32[8,8]{1,0:T(8,128)} %i_hbm.1, f32[8,8]{1,0:T(8,128)} %p_hbm.1), custom_call_target="tpu_custom_call" | custom-call | bytes 4096 | tf_op jit(solution)/shard_map/pack/pallas_call | solution.py:32
  4.9 0.1 collective-permute-start.1
  5.0 5.2 %fetch.4 = (bf16[8,128]{1,0:T(8,128)(2,1)S(1)}, s32[8,128]{1,0:T(8,128)S(1)}, bf16[2048,3584]{1,0:T(8,128)(2,1)S(1)}, bf16[8,7168]{1,0:T(8,128)(2,1)S(1)}) custom-call(bf16[8,128]{1,0:T(8,128)(2,1)S(1)} %pack.1.refs_0_, s32[8,128]{1,0:T(8,128)S(1)} %broadcast_in_dim.3.refs_1_, bf16[2048,7168]{1,0:T(8,128)(2,1)} %refs_2_.6, bf16[8,7168]{1,0:T(8,128)(2,1)} %refs_3_.3), custom_call_target="tpu_custom_call" | custom-call | bytes 14794752 | tf_op jit(solution)/shard_map/fetch/pallas_call | solution.py:32
  10.2 0.0 collective-permute-done.1.refs_3_
  10.2 0.0 collective-permute-done.refs_2_
  10.2 1.9 %collective-permute-start.3 = (bf16[16,3712]{1,0:T(8,128)(2,1)S(1)}, bf16[16,3712]{1,0:T(8,128)(2,1)S(1)}, u32[]{:S(2)}, u32[]{:S(2)}) collective-permute-start(bf16[16,3712]{1,0:T(8,128)(2,1)S(1)} %get-tuple-element.46.refs_1_), channel_id=1, source_target_pairs={{0,2},{1,3},{2,0},{3,1},{4,6},{5,7},{6,4},{7,5},{8,10},{9,11},{10,... | collective-permute-start | bytes 356360 | tf_op jit(solution)/shard_map/ppermute | solution.py:22
  12.1 1.6 %collective-permute-start.2 = (bf16[16,3584]{1,0:T(8,128)(2,1)S(1)}, bf16[16,3584]{1,0:T(8,128)(2,1)S(1)}, u32[]{:S(2)}, u32[]{:S(2)}) collective-permute-start(bf16[16,3584]{1,0:T(8,128)(2,1)S(1)} %get-tuple-element.45.refs_0_), channel_id=1, source_target_pairs={{0,4},{1,5},{2,6},{3,7},{4,0},{5,1},{6,2},{7,3},{8,12},{9,13},{10,... | collective-permute-start | bytes 344072 | tf_op jit(solution)/shard_map/ppermute | solution.py:22
  13.7 3.5 %fetch.5 = (bf16[16,3584]{1,0:T(8,128)(2,1)S(1)}, bf16[16,3712]{1,0:T(8,128)(2,1)S(1)}, bf16[1024,2048]{1,0:T(8,128)(2,1)S(1)}, bf16[1024,2048]{1,0:T(8,128)(2,1)S(1)}) custom-call(bf16[16,3584]{1,0:T(8,128)(2,1)S(1)} %get-tuple-element.45.refs_0_, bf16[16,3712]{1,0:T(8,128)(2,1)S(1)} %get-tuple-element.46.refs_1_, bf16[7168,2048]{1,0:T(8,128)(2,1)} %refs_12_.1, ...), custom_call_target="tpu_custom_call" | custom-call | bytes 8388608 | tf_op jit(solution)/shard_map/fetch/pallas_call | solution.py:32
  17.2 0.0 collective-permute-done.2.refs_1_
  17.2 0.0 collective-permute-done.3.refs_3_
  17.2 1.3 %collective-permute-start.5 = (bf16[32,3712]{1,0:T(8,128)(2,1)S(1)}, bf16[32,3712]{1,0:T(8,128)(2,1)S(1)}, u32[]{:S(2)}, u32[]{:S(2)}) collective-permute-start(bf16[32,3712]{1,0:T(8,128)(2,1)S(1)} %get-tuple-element.50.refs_1_), channel_id=1, source_target_pairs={{0,4},{1,5},{2,6},{3,7},{4,0},{5,1},{6,2},{7,3},{8,12},{9,13},{10,... | collective-permute-start | bytes 712712 | tf_op jit(solution)/shard_map/ppermute | solution.py:22
  18.6 0.5 collective-permute-start.4
  19.1 5.2 %fetch.6 = (bf16[32,3584]{1,0:T(8,128)(2,1)S(1)}, bf16[32,3712]{1,0:T(8,128)(2,1)S(1)}, bf16[2048,3584]{1,0:T(8,128)(2,1)S(1)}) custom-call(bf16[32,3584]{1,0:T(8,128)(2,1)S(1)} %get-tuple-element.49.refs_0_, bf16[32,3712]{1,0:T(8,128)(2,1)S(1)} %get-tuple-element.50.refs_1_, bf16[2048,7168]{1,0:T(8,128)(2,1)} %refs_2_.6), custom_call_target="tpu_custom_call" | custom-call | bytes 14680064 | tf_op jit(solution)/shard_map/fetch/pallas_call | solution.py:32
  24.3 0.1 collective-permute-start.8
  24.4 0.0 collective-permute-done.5.refs_1_
  24.4 0.5 collective-permute-start.9
  24.9 0.1 collective-permute-start.6
  25.0 0.0 collective-permute-done.4.refs_0_
  25.0 0.4 collective-permute-start.7
  25.4 2.2 %fetch.7 = (bf16[32,3584]{1,0:T(8,128)(2,1)S(1)}, bf16[32,3712]{1,0:T(8,128)(2,1)S(1)}, bf16[512,2048]{1,0:T(8,128)(2,1)S(1)}, bf16[512,2048]{1,0:T(8,128)(2,1)S(1)}) custom-call(bf16[32,3584]{1,0:T(8,128)(2,1)S(1)} %collective-permute-done.4.refs_0_, bf16[32,3712]{1,0:T(8,128)(2,1)S(1)} %collective-permute-done.5.refs_1_, bf16[7168,2048]{1,0:T(8,128)(2,1)} %refs_12_.1, ...), custom_call_target="tpu_custom_call" | custom-call | bytes 4194304 | tf_op jit(solution)/shard_map/fetch/pallas_call | solution.py:32
  27.6 0.0 collective-permute-done.6.refs_2_
  27.6 0.0 collective-permute-done.8.refs_6_
  27.7 0.0 collective-permute-done.7.refs_3_
  27.7 0.0 collective-permute-done.9.refs_7_
  27.7 15.5 %gate_up.1 = (bf16[128,2048]{1,0:T(8,128)(2,1)S(1)}, f32[128,128]{1,0:T(8,128)S(1)}) custom-call(s32[8,128]{1,0:T(8,128)S(1)} %get-tuple-element.42.own_ref, bf16[32,3584]{1,0:T(8,128)(2,1)S(1)} %get-tuple-element.51.refs_0_, bf16[32,3584]{1,0:T(8,128)(2,1)S(1)} %get-tuple-element.52.refs_1_, bf16[32,3584]{1,0:T(8,128)(2,1)S(1)} %collective-permute-done.6.refs_2_, ...), custom_call_target="tpu_custom_call" | custom-call | flops 7516192768 | bytes 46137344 | tf_op jit(solution)/shard_map/gate_up/pallas_call | solution.py:32
  43.2 2.1 %down.3 = (f32[64,3584]{1,0:T(8,128)S(1)}, bf16[64,3584]{1,0:T(8,128)(2,1)S(1)}) custom-call(bf16[128,2048]{1,0:T(8,128)(2,1)S(1)} %get-tuple-element.59.h_ref, f32[128,128]{1,0:T(8,128)S(1)} %get-tuple-element.60.w_ref, bf16[2048,3584]{1,0:T(8,128)(2,1)S(1)} %get-tuple-element.70.d_ref), custom_call_target="tpu_custom_call" | custom-call | flops 1879048192 | bytes 458752 | tf_op jit(solution)/shard_map/down/pallas_call | solution.py:32
  45.3 0.2 collective-permute-start.14
  45.4 2.1 %down.2 = (f32[64,3584]{1,0:T(8,128)S(1)}, bf16[64,3584]{1,0:T(8,128)(2,1)S(1)}) custom-call(bf16[128,2048]{1,0:T(8,128)(2,1)S(1)} %get-tuple-element.59.h_ref, f32[128,128]{1,0:T(8,128)S(1)} %get-tuple-element.60.w_ref, bf16[2048,3584]{1,0:T(8,128)(2,1)S(1)} %get-tuple-element.61.d_ref), custom_call_target="tpu_custom_call" | custom-call | flops 1879048192 | bytes 458752 | tf_op jit(solution)/shard_map/down/pallas_call | solution.py:32
  47.5 0.5 collective-permute-start.10
  48.0 0.0 collective-permute-done.14.refs_1_
  48.0 0.1 add.11
  48.1 0.8 %collective-permute-start.15 = (bf16[32,3584]{1,0:T(8,128)(2,1)S(1)}, bf16[32,3584]{1,0:T(8,128)(2,1)S(1)}, u32[]{:S(2)}, u32[]{:S(2)}) collective-permute-start(bf16[32,3584]{1,0:T(8,128)(2,1)S(1)} %get-tuple-element.74), channel_id=1, source_target_pairs={{0,4},{1,5},{2,6},{3,7},{4,0},{5,1},{6,2},{7,3},{8,12},{9,13},{10,... | collective-permute-start | bytes 688136 | tf_op jit(solution)/shard_map/ppermute | solution.py:22
  48.9 0.5 collective-permute-done.10.refs_1_
  49.4 0.1 add.8
  49.5 1.6 %collective-permute-start.11 = (bf16[32,3584]{1,0:T(8,128)(2,1)S(1)}, bf16[32,3584]{1,0:T(8,128)(2,1)S(1)}, u32[]{:S(2)}, u32[]{:S(2)}) collective-permute-start(bf16[32,3584]{1,0:T(8,128)(2,1)S(1)} %get-tuple-element.65), channel_id=1, source_target_pairs={{0,2},{1,3},{2,0},{3,1},{4,6},{5,7},{6,4},{7,5},{8,10},{9,11},{10,... | collective-permute-start | bytes 688136 | tf_op jit(solution)/shard_map/ppermute | solution.py:22
  51.1 4.6 %collective-permute-done.15.refs_1_ = bf16[32,3584]{1,0:T(8,128)(2,1)S(1)} collective-permute-done((bf16[32,3584]{1,0:T(8,128)(2,1)S(1)}, bf16[32,3584]{1,0:T(8,128)(2,1)S(1)}, u32[]{:S(2)}, u32[]{:S(2)}) %collective-permute-start.15) | collective-permute-done | bytes 229408 | tf_op jit(solution)/shard_map/ppermute | solution.py:22
  55.8 1.6 %collective-permute-start.16 = (bf16[16,3584]{1,0:T(8,128)(2,1)S(1)}, bf16[16,3584]{1,0:T(8,128)(2,1)S(1)}, u32[]{:S(2)}, u32[]{:S(2)}) collective-permute-start(bf16[16,3584]{1,0:T(8,128)(2,1)S(1)} %get-tuple-element.76), channel_id=1, source_target_pairs={{0,2},{1,3},{2,0},{3,1},{4,6},{5,7},{6,4},{7,5},{8,10},{9,11},{10,... | collective-permute-start | bytes 344072 | tf_op jit(solution)/shard_map/ppermute | solution.py:22
  57.3 0.1 collective-permute-done.11.refs_1_
  57.5 0.8 %collective-permute-start.12 = (bf16[16,3584]{1,0:T(8,128)(2,1)S(1)}, bf16[16,3584]{1,0:T(8,128)(2,1)S(1)}, u32[]{:S(2)}, u32[]{:S(2)}) collective-permute-start(bf16[16,3584]{1,0:T(8,128)(2,1)S(1)} %get-tuple-element.67), channel_id=1, source_target_pairs={{0,4},{1,5},{2,6},{3,7},{4,0},{5,1},{6,2},{7,3},{8,12},{9,13},{10,... | collective-permute-start | bytes 344072 | tf_op jit(solution)/shard_map/ppermute | solution.py:22
  58.3 2.3 %collective-permute-done.16.refs_1_ = bf16[16,3584]{1,0:T(8,128)(2,1)S(1)} collective-permute-done((bf16[16,3584]{1,0:T(8,128)(2,1)S(1)}, bf16[16,3584]{1,0:T(8,128)(2,1)S(1)}, u32[]{:S(2)}, u32[]{:S(2)}) %collective-permute-start.16) | collective-permute-done | bytes 114720 | tf_op jit(solution)/shard_map/ppermute | solution.py:22
  60.7 2.7 %collective-permute-start.17 = (bf16[8,3584]{1,0:T(8,128)(2,1)S(1)}, bf16[8,3584]{1,0:T(8,128)(2,1)S(1)}, u32[]{:S(2)}, u32[]{:S(2)}) collective-permute-start(bf16[8,3584]{1,0:T(8,128)(2,1)S(1)} %get-tuple-element.78), channel_id=1, source_target_pairs={{0,8},{1,9},{2,10},{3,11},{4,12},{5,13},{6,14},{7,15},{8,0},{9,1},... | collective-permute-start | bytes 172040 | tf_op jit(solution)/shard_map/ppermute | solution.py:22
  63.3 0.0 collective-permute-done.12.refs_1_
  63.4 2.1 %collective-permute-start.13 = (bf16[8,3584]{1,0:T(8,128)(2,1)S(1)}, bf16[8,3584]{1,0:T(8,128)(2,1)S(1)}, u32[]{:S(2)}, u32[]{:S(2)}) collective-permute-start(bf16[8,3584]{1,0:T(8,128)(2,1)S(1)} %get-tuple-element.69), channel_id=1, source_target_pairs={{0,8},{1,9},{2,10},{3,11},{4,12},{5,13},{6,14},{7,15},{8,0},{9,1},... | collective-permute-start | bytes 172040 | tf_op jit(solution)/shard_map/ppermute | solution.py:22
  65.5 1.8 %collective-permute-done.17.refs_3_ = bf16[8,3584]{1,0:T(8,128)(2,1)S(1)} collective-permute-done((bf16[8,3584]{1,0:T(8,128)(2,1)S(1)}, bf16[8,3584]{1,0:T(8,128)(2,1)S(1)}, u32[]{:S(2)}, u32[]{:S(2)}) %collective-permute-start.17) | collective-permute-done | bytes 57376 | tf_op jit(solution)/shard_map/ppermute | solution.py:22
  67.2 1.9 %collective-permute-done.13.refs_1_ = bf16[8,3584]{1,0:T(8,128)(2,1)S(1)} collective-permute-done((bf16[8,3584]{1,0:T(8,128)(2,1)S(1)}, bf16[8,3584]{1,0:T(8,128)(2,1)S(1)}, u32[]{:S(2)}, u32[]{:S(2)}) %collective-permute-start.13) | collective-permute-done | bytes 57376 | tf_op jit(solution)/shard_map/ppermute | solution.py:22
  69.1 0.7 add.14
  (7 shorter events, 0.2 us)
Async XLA Ops:
  0.0 10.2 %collective-permute-start = (bf16[8,7168]{1,0:T(8,128)(2,1)}, bf16[8,7168]{1,0:T(8,128)(2,1)S(1)}, u32[]{:S(2)}, u32[]{:S(2)}) collective-permute-start(bf16[8,7168]{1,0:T(8,128)(2,1)} %refs_3_.3), channel_id=1, source_target_pairs={{0,8},{1,9},{2,10},{3,11},{4,12},{5,13},{6,14},{7,15},{8,0},{9,1},... | collective-permute-start | bytes 344072 | tf_op jit(solution)/shard_map/ppermute | solution.py:22
  4.9 5.3 %collective-permute-start.1 = (bf16[8,128]{1,0:T(8,128)(2,1)S(1)}, bf16[8,128]{1,0:T(8,128)(2,1)S(1)}, u32[]{:S(2)}, u32[]{:S(2)}) collective-permute-start(bf16[8,128]{1,0:T(8,128)(2,1)S(1)} %pack.1.refs_0_), channel_id=1, source_target_pairs={{0,8},{1,9},{2,10},{3,11},{4,12},{5,13},{6,14},{7,15},{8,0},{9,1},... | collective-permute-start | bytes 6152 | tf_op jit(solution)/shard_map/ppermute | solution.py:22
  10.2 6.9 %collective-permute-start.3 = (bf16[16,3712]{1,0:T(8,128)(2,1)S(1)}, bf16[16,3712]{1,0:T(8,128)(2,1)S(1)}, u32[]{:S(2)}, u32[]{:S(2)}) collective-permute-start(bf16[16,3712]{1,0:T(8,128)(2,1)S(1)} %get-tuple-element.46.refs_1_), channel_id=1, source_target_pairs={{0,2},{1,3},{2,0},{3,1},{4,6},{5,7},{6,4},{7,5},{8,10},{9,11},{10,... | collective-permute-start | bytes 356360 | tf_op jit(solution)/shard_map/ppermute | solution.py:22
  12.1 5.1 %collective-permute-start.2 = (bf16[16,3584]{1,0:T(8,128)(2,1)S(1)}, bf16[16,3584]{1,0:T(8,128)(2,1)S(1)}, u32[]{:S(2)}, u32[]{:S(2)}) collective-permute-start(bf16[16,3584]{1,0:T(8,128)(2,1)S(1)} %get-tuple-element.45.refs_0_), channel_id=1, source_target_pairs={{0,4},{1,5},{2,6},{3,7},{4,0},{5,1},{6,2},{7,3},{8,12},{9,13},{10,... | collective-permute-start | bytes 344072 | tf_op jit(solution)/shard_map/ppermute | solution.py:22
  17.2 7.2 %collective-permute-start.5 = (bf16[32,3712]{1,0:T(8,128)(2,1)S(1)}, bf16[32,3712]{1,0:T(8,128)(2,1)S(1)}, u32[]{:S(2)}, u32[]{:S(2)}) collective-permute-start(bf16[32,3712]{1,0:T(8,128)(2,1)S(1)} %get-tuple-element.50.refs_1_), channel_id=1, source_target_pairs={{0,4},{1,5},{2,6},{3,7},{4,0},{5,1},{6,2},{7,3},{8,12},{9,13},{10,... | collective-permute-start | bytes 712712 | tf_op jit(solution)/shard_map/ppermute | solution.py:22
  18.6 6.4 %collective-permute-start.4 = (bf16[32,3584]{1,0:T(8,128)(2,1)S(1)}, bf16[32,3584]{1,0:T(8,128)(2,1)S(1)}, u32[]{:S(2)}, u32[]{:S(2)}) collective-permute-start(bf16[32,3584]{1,0:T(8,128)(2,1)S(1)} %get-tuple-element.49.refs_0_), channel_id=1, source_target_pairs={{0,2},{1,3},{2,0},{3,1},{4,6},{5,7},{6,4},{7,5},{8,10},{9,11},{10,... | collective-permute-start | bytes 688136 | tf_op jit(solution)/shard_map/ppermute | solution.py:22
  24.3 3.4 %collective-permute-start.8 = (bf16[32,3712]{1,0:T(8,128)(2,1)S(1)}, bf16[32,3712]{1,0:T(8,128)(2,1)S(1)}, u32[]{:S(2)}, u32[]{:S(2)}) collective-permute-start(bf16[32,3712]{1,0:T(8,128)(2,1)S(1)} %get-tuple-element.53.refs_4_), channel_id=1, source_target_pairs={{0,1},{1,0},{2,3},{3,2},{4,5},{5,4},{6,7},{7,6},{8,9},{9,8},{10,11... | collective-permute-start | bytes 712712 | tf_op jit(solution)/shard_map/ppermute | solution.py:22
  24.4 3.3 %collective-permute-start.9 = (bf16[32,3712]{1,0:T(8,128)(2,1)S(1)}, bf16[32,3712]{1,0:T(8,128)(2,1)S(1)}, u32[]{:S(2)}, u32[]{:S(2)}) collective-permute-start(bf16[32,3712]{1,0:T(8,128)(2,1)S(1)} %collective-permute-done.5.refs_1_), channel_id=1, source_target_pairs={{0,1},{1,0},{2,3},{3,2},{4,5},{5,4},{6,7},{7,6},{8,9},{9,8},{10,11... | collective-permute-start | bytes 712712 | tf_op jit(solution)/shard_map/ppermute | solution.py:22
  24.9 2.8 %collective-permute-start.6 = (bf16[32,3584]{1,0:T(8,128)(2,1)S(1)}, bf16[32,3584]{1,0:T(8,128)(2,1)S(1)}, u32[]{:S(2)}, u32[]{:S(2)}) collective-permute-start(bf16[32,3584]{1,0:T(8,128)(2,1)S(1)} %get-tuple-element.51.refs_0_), channel_id=1, source_target_pairs={{0,1},{1,0},{2,3},{3,2},{4,5},{5,4},{6,7},{7,6},{8,9},{9,8},{10,11... | collective-permute-start | bytes 688136 | tf_op jit(solution)/shard_map/ppermute | solution.py:22
  25.0 2.7 %collective-permute-start.7 = (bf16[32,3584]{1,0:T(8,128)(2,1)S(1)}, bf16[32,3584]{1,0:T(8,128)(2,1)S(1)}, u32[]{:S(2)}, u32[]{:S(2)}) collective-permute-start(bf16[32,3584]{1,0:T(8,128)(2,1)S(1)} %collective-permute-done.4.refs_0_), channel_id=1, source_target_pairs={{0,1},{1,0},{2,3},{3,2},{4,5},{5,4},{6,7},{7,6},{8,9},{9,8},{10,11... | collective-permute-start | bytes 688136 | tf_op jit(solution)/shard_map/ppermute | solution.py:22
  45.3 2.7 %collective-permute-start.14 = (bf16[64,3584]{1,0:T(8,128)(2,1)S(1)}, bf16[64,3584]{1,0:T(8,128)(2,1)S(1)}, u32[]{:S(2)}, u32[]{:S(2)}) collective-permute-start(bf16[64,3584]{1,0:T(8,128)(2,1)S(1)} %get-tuple-element.72), channel_id=1, source_target_pairs={{0,1},{1,0},{2,3},{3,2},{4,5},{5,4},{6,7},{7,6},{8,9},{9,8},{10,11... | collective-permute-start | bytes 1376264 | tf_op jit(solution)/shard_map/ppermute | solution.py:22
  47.5 1.9 %collective-permute-start.10 = (bf16[64,3584]{1,0:T(8,128)(2,1)S(1)}, bf16[64,3584]{1,0:T(8,128)(2,1)S(1)}, u32[]{:S(2)}, u32[]{:S(2)}) collective-permute-start(bf16[64,3584]{1,0:T(8,128)(2,1)S(1)} %get-tuple-element.63), channel_id=1, source_target_pairs={{0,1},{1,0},{2,3},{3,2},{4,5},{5,4},{6,7},{7,6},{8,9},{9,8},{10,11... | collective-permute-start | bytes 1376264 | tf_op jit(solution)/shard_map/ppermute | solution.py:22
  48.1 7.7 %collective-permute-start.15 = (bf16[32,3584]{1,0:T(8,128)(2,1)S(1)}, bf16[32,3584]{1,0:T(8,128)(2,1)S(1)}, u32[]{:S(2)}, u32[]{:S(2)}) collective-permute-start(bf16[32,3584]{1,0:T(8,128)(2,1)S(1)} %get-tuple-element.74), channel_id=1, source_target_pairs={{0,4},{1,5},{2,6},{3,7},{4,0},{5,1},{6,2},{7,3},{8,12},{9,13},{10,... | collective-permute-start | bytes 688136 | tf_op jit(solution)/shard_map/ppermute | solution.py:22
  49.5 7.9 %collective-permute-start.11 = (bf16[32,3584]{1,0:T(8,128)(2,1)S(1)}, bf16[32,3584]{1,0:T(8,128)(2,1)S(1)}, u32[]{:S(2)}, u32[]{:S(2)}) collective-permute-start(bf16[32,3584]{1,0:T(8,128)(2,1)S(1)} %get-tuple-element.65), channel_id=1, source_target_pairs={{0,2},{1,3},{2,0},{3,1},{4,6},{5,7},{6,4},{7,5},{8,10},{9,11},{10,... | collective-permute-start | bytes 688136 | tf_op jit(solution)/shard_map/ppermute | solution.py:22
  55.8 4.9 %collective-permute-start.16 = (bf16[16,3584]{1,0:T(8,128)(2,1)S(1)}, bf16[16,3584]{1,0:T(8,128)(2,1)S(1)}, u32[]{:S(2)}, u32[]{:S(2)}) collective-permute-start(bf16[16,3584]{1,0:T(8,128)(2,1)S(1)} %get-tuple-element.76), channel_id=1, source_target_pairs={{0,2},{1,3},{2,0},{3,1},{4,6},{5,7},{6,4},{7,5},{8,10},{9,11},{10,... | collective-permute-start | bytes 344072 | tf_op jit(solution)/shard_map/ppermute | solution.py:22
  57.5 5.8 %collective-permute-start.12 = (bf16[16,3584]{1,0:T(8,128)(2,1)S(1)}, bf16[16,3584]{1,0:T(8,128)(2,1)S(1)}, u32[]{:S(2)}, u32[]{:S(2)}) collective-permute-start(bf16[16,3584]{1,0:T(8,128)(2,1)S(1)} %get-tuple-element.67), channel_id=1, source_target_pairs={{0,4},{1,5},{2,6},{3,7},{4,0},{5,1},{6,2},{7,3},{8,12},{9,13},{10,... | collective-permute-start | bytes 344072 | tf_op jit(solution)/shard_map/ppermute | solution.py:22
  60.7 6.6 %collective-permute-start.17 = (bf16[8,3584]{1,0:T(8,128)(2,1)S(1)}, bf16[8,3584]{1,0:T(8,128)(2,1)S(1)}, u32[]{:S(2)}, u32[]{:S(2)}) collective-permute-start(bf16[8,3584]{1,0:T(8,128)(2,1)S(1)} %get-tuple-element.78), channel_id=1, source_target_pairs={{0,8},{1,9},{2,10},{3,11},{4,12},{5,13},{6,14},{7,15},{8,0},{9,1},... | collective-permute-start | bytes 172040 | tf_op jit(solution)/shard_map/ppermute | solution.py:22
  63.4 5.8 %collective-permute-start.13 = (bf16[8,3584]{1,0:T(8,128)(2,1)S(1)}, bf16[8,3584]{1,0:T(8,128)(2,1)S(1)}, u32[]{:S(2)}, u32[]{:S(2)}) collective-permute-start(bf16[8,3584]{1,0:T(8,128)(2,1)S(1)} %get-tuple-element.69), channel_id=1, source_target_pairs={{0,8},{1,9},{2,10},{3,11},{4,12},{5,13},{6,14},{7,15},{8,0},{9,1},... | collective-permute-start | bytes 172040 | tf_op jit(solution)/shard_map/ppermute | solution.py:22
